TPU v7x, 256 devices: a whole 4x4x8 slice. The times are simulated.
256 devices in a mesh: heads: 8 (over z), tokens: 32 (over x, y, core).
Axes of the slice: x: 4, y: 4, z: 8, core: 2. Of those that a mesh axis runs over, the one named last changes fastest.
Arguments:
- hidden_in: bfloat16 [8192, 5120], P('tokens', 'heads'), may hold values from -4 to 4
- queries: bfloat16 [8192, 5120], P('tokens', 'heads'), may hold values from -7 to 7
- keyvals: bfloat16 [8192, 2, 1024], P('tokens', None, 'heads'), may hold values from -6 to 6
- out_weight: bfloat16 [5120, 5120], P('heads', 'tokens'), may hold values from -0.01953125 to 0.01953125
- kv_gain: bfloat16 [5120], P('heads'), may hold values from 0.099609375 to 1.8984375
- kv_weight: bfloat16 [5120, 2, 1024], P(None, None, 'heads'), may hold values from -0.25 to 0.25
- cache: bfloat16 [131072, 2, 1024], P('tokens', None, 'heads'), may hold values from -12 to 12
- page_home: int32 [512], replicated, may hold values from 0 to 8191, as said below
- cache_len: int32 [1], replicated, may hold values from 16384 to 65536
- beam_state: bfloat16 [256, 5120], P(None, 'tokens'), may hold values from -4 to 4
- parents: int32 [256], replicated, may hold values from 0 to 255
- beam_gain: bfloat16 [2, 5120], P(None, 'tokens'), may hold values from 0.099609375 to 1.8984375
- query_weight: bfloat16 [2, 5120, 5120], P(None, 'tokens', 'heads'), may hold values from -1 to 1
- beam_out_weight: bfloat16 [2, 5120, 5120], P(None, 'heads', 'tokens'), may hold values from -0.078125 to 0.078125
Outputs:
- stretch_hidden: bfloat16 [8192, 5120], P('tokens', 'heads')
- new_cache: bfloat16 [131072, 2, 1024], P('tokens', None, 'heads')
- beams_out: bfloat16 [256, 5120], P(None, 'tokens')
Inputs may be any that keep to these rules, and one draw needn't show every extreme that they name: Prefill page p overwrites a page held by index (p + c) mod 32 of tokens, i.e. page_home[p] // 256 equals it, for one c of each draw; all entries differ.
All inputs are finite; a program needn't handle non-finite values.
Results may differ from a plain program's by a relative error of at most 0.023.
Values may be sent and summed in bfloat16 or wider, within the bound.
A program may use at most 128 MiB of HBM per device.

v0:
```python
import jax
import jax.numpy as jnp
from jax import lax
from jax.sharding import Mesh
from jax.sharding import PartitionSpec as P

D = 5120
DH = 128
WINDOW = 1024
PAGE = 16
LAYERS = 2
TOKENS = ("tokens_0", "tokens_1", "tokens_2")


epsilon = 1e-06


def passed_along(value, axis, steps):
    count = lax.axis_size(axis)
    initial, last = (max(0, -steps), min(count, count - steps))
    return lax.ppermute(value, axis, [(source, source + steps) for source in range(initial, last)])


def sent_together(arrays, axis, dim, along):
    widths = [a.shape[along] for a in arrays]
    both = jnp.concatenate(arrays, axis=along)
    out = lax.all_gather(both, axis, axis=dim, tiled=True)
    return tuple(jnp.split(out, [sum(widths[:k]) for k in range(1, len(widths))], axis=along))


def copy_for_each(array, axis):
    copies = jnp.broadcast_to(array, (lax.axis_size(axis), *array.shape))
    return lax.all_to_all(copies, axis, split_axis=0, concat_axis=0, tiled=True)


def over_copies(array, axis):
    everything = copy_for_each(array, axis)
    return jnp.sum(everything, axis=0)


def cut_along(array, dim, devices):
    before, after = (array.shape[:dim], array.shape[dim + 1 :])
    return jnp.moveaxis(array.reshape(*before, devices, -1, *after), dim, 0)


def sent_and_summed(array, axis, dim):
    parts = cut_along(array, dim, lax.axis_size(axis))
    arrived = lax.all_to_all(parts, axis, split_axis=0, concat_axis=0, tiled=True)
    return arrived.sum(axis=0)


def sum_in_two_steps(array, axes, dim):
    far, near = axes
    own = sent_and_summed(cut_along(array, dim, lax.axis_size(far)), near, dim + 1)
    return jnp.sum(lax.all_to_all(own, far, 0, 0, tiled=True), axis=0)


def rows_for(lines, devices):
    spare = -len(lines) % devices
    return jnp.pad(lines, [(0, spare)] + [(0, 0)] * (lines.ndim - 1))


def joined_along(parts, dim):
    lengths = list(parts.shape[1:])
    lengths[dim] *= parts.shape[0]
    return jnp.moveaxis(parts, 0, dim).reshape(lengths)


def whole_of(array, axes, dim):
    far, near = axes
    initial = copy_for_each(array, far)
    parts = jnp.swapaxes(copy_for_each(initial, near), 0, 1)
    return joined_along(parts.reshape(-1, *array.shape), dim)


def total_of(array, axes):
    lines = array.reshape(-1, array.shape[-1])
    own = sum_in_two_steps(
        rows_for(lines, lax.axis_size(axes[0]) * lax.axis_size(axes[1])), axes, 0
    )
    whole = whole_of(own, axes, 0)
    return whole[: len(lines)].reshape(array.shape)


def taken_together(array, axis):
    everything = copy_for_each(array, axis)
    return jnp.max(everything, axis=0)


def total_of_2(array, axes):
    own = sum_in_two_steps(
        rows_for(array, lax.axis_size(axes[0]) * lax.axis_size(axes[1])), axes, 0
    )
    whole = whole_of(own, axes, 0)
    return whole[: len(array)].reshape(array.shape)


def together(arrays, axis):
    flat, at, outs = (jnp.concatenate([a.reshape(-1) for a in arrays]), 0, [])
    subtotal = total_of_2(flat, axis)
    for a in arrays:
        outs.append(subtotal[at : at + a.size].reshape(a.shape))
        at += a.size
    return tuple(outs)


def shards(
    hidden_in,
    queries,
    keyvals,
    out_weight,
    kv_gain,
    kv_weight,
    cache,
    page_home,
    cache_len,
    beam_state,
    parents,
    beam_gain,
    query_weight,
    beam_out_weight,
):
    tok_rows = hidden_in.shape[0]
    kv_local = keyvals.shape[2] // DH
    head_local = queries.shape[1] // DH
    group_size = head_local // kv_local
    score_scale = DH ** (-0.5)
    place_index = lax.axis_index(TOKENS)
    reach_back = -(-WINDOW // tok_rows)
    window_rows = keyvals
    shard_count = 1
    while shard_count < reach_back + 1:
        arrived_rows = passed_along(window_rows, TOKENS, shard_count)
        window_rows = jnp.concatenate([arrived_rows, window_rows], axis=0)
        shard_count = shard_count * 2
    window_rows = window_rows[window_rows.shape[0] - (reach_back + 1) * tok_rows :]
    query_block = queries.reshape(tok_rows, kv_local, group_size, DH)
    key_block = window_rows[:, 0].reshape(-1, kv_local, DH)
    value_block = window_rows[:, 1].reshape(-1, kv_local, DH)
    scores = (
        jnp.einsum("tkgd,skd->kgts", query_block, key_block, preferred_element_type=jnp.float32)
        * score_scale
    )
    query_pos = place_index * tok_rows + jnp.arange(tok_rows, dtype=jnp.int32)
    key_pos = (place_index - reach_back) * tok_rows + jnp.arange(
        window_rows.shape[0], dtype=jnp.int32
    )
    allowed = (
        (key_pos[None, :] <= query_pos[:, None])
        & (key_pos[None, :] > query_pos[:, None] - WINDOW)
        & (key_pos[None, :] >= 0)
    )
    scores = jnp.where(allowed, scores, -1e30)
    highest = jnp.max(scores, axis=-1, keepdims=True)
    expo = jnp.exp(scores - highest)
    weights = (expo / jnp.sum(expo, axis=-1, keepdims=True)).astype(jnp.bfloat16)
    attended = jnp.einsum(
        "kgts,skd->tkgd", weights, value_block, preferred_element_type=jnp.float32
    )
    attended = attended.astype(jnp.bfloat16).reshape(tok_rows, head_local * DH)
    partial_out = jnp.dot(
        attended,
        lax.all_gather(out_weight, TOKENS, axis=1, tiled=True),
        preferred_element_type=jnp.float32,
    )
    head_total = lax.psum_scatter(partial_out, "heads", scatter_dimension=1, tiled=True)
    stretch_hidden = (hidden_in.astype(jnp.float32) + head_total).astype(jnp.bfloat16)
    full_hidden, full_gain = sent_together((stretch_hidden, kv_gain[None, :]), "heads", 1, 0)
    hidden_f = full_hidden.astype(jnp.float32)
    factor = lax.rsqrt(jnp.mean(hidden_f * hidden_f, axis=1) + epsilon)
    full_rows = (hidden_f * factor[:, None] * full_gain.astype(jnp.float32)).astype(jnp.bfloat16)
    fresh = jnp.dot(
        full_rows, kv_weight.reshape(kv_weight.shape[0], -1), preferred_element_type=jnp.float32
    ).astype(jnp.bfloat16)
    page_width = PAGE * fresh.shape[1]
    own_pages = tok_rows // PAGE
    peer_count = lax.axis_size(TOKENS)
    capacity = -(-own_pages // peer_count)
    pages_here = cache.shape[0] // PAGE
    page_rows = fresh.reshape(own_pages, page_width)
    mine = lax.dynamic_slice_in_dim(page_home, place_index * own_pages, own_pages, 0)
    target = mine // pages_here * capacity + jnp.arange(own_pages, dtype=jnp.int32) // peer_count
    outbox_map = (
        jnp.arange(peer_count * capacity, dtype=jnp.int32)[:, None] == target[None, :]
    ).astype(jnp.bfloat16)
    outbox = jnp.dot(outbox_map, page_rows, preferred_element_type=jnp.float32).astype(jnp.bfloat16)
    inbox = lax.all_to_all(
        outbox.reshape(peer_count, capacity, page_width),
        TOKENS,
        split_axis=0,
        concat_axis=0,
        tiled=True,
    )
    inbox = inbox.reshape(peer_count * capacity, page_width)
    every_page = jnp.arange(page_home.shape[0], dtype=jnp.int32)
    source_slot = every_page // own_pages * capacity + every_page % own_pages // peer_count
    landing = jnp.where(page_home // pages_here == place_index, page_home % pages_here, -1)
    land_map = (jnp.arange(pages_here, dtype=jnp.int32)[:, None] == landing[None, :]).astype(
        jnp.bfloat16
    )
    slot_map = (
        source_slot[:, None] == jnp.arange(peer_count * capacity, dtype=jnp.int32)[None, :]
    ).astype(jnp.bfloat16)
    chosen = jnp.dot(land_map, slot_map, preferred_element_type=jnp.float32)
    written = jnp.sum(chosen, axis=1) > 0.5
    arrived_pages = jnp.dot(
        chosen.astype(jnp.bfloat16), inbox, preferred_element_type=jnp.float32
    ).astype(jnp.bfloat16)
    new_cache = jnp.where(
        written[:, None], arrived_pages, cache.reshape(pages_here, page_width)
    ).reshape(cache.shape)
    cache_rows = cache.shape[0]
    row_ids = place_index * cache_rows + jnp.arange(cache_rows, dtype=jnp.int32)
    live_rows = (row_ids < cache_len[0]) | jnp.repeat(written, PAGE)
    cache_keys = new_cache[:, 0].reshape(cache_rows, kv_local, DH)
    cache_values = new_cache[:, 1].reshape(cache_rows, kv_local, DH)
    beam_rows = parents.shape[0]
    state = jnp.take(beam_state, parents, axis=0)
    for layer_index in range(LAYERS):
        state_f = state.astype(jnp.float32)
        squares = over_copies(jnp.sum(state_f * state_f, axis=1), TOKENS)
        factor = lax.rsqrt(squares / D + epsilon)
        normed = (
            state_f * factor[:, None] * beam_gain[layer_index].astype(jnp.float32)[None, :]
        ).astype(jnp.bfloat16)
        query_part = jnp.dot(normed, query_weight[layer_index], preferred_element_type=jnp.float32)
        query_rows = total_of(query_part, (("tokens_0", "tokens_1"), "tokens_2")).astype(
            jnp.bfloat16
        )
        query_rows = query_rows.reshape(beam_rows, kv_local, group_size, DH)
        cross_scores = (
            jnp.einsum("bkgd,skd->kgbs", query_rows, cache_keys, preferred_element_type=jnp.float32)
            * score_scale
        )
        cross_scores = jnp.where(live_rows, cross_scores, -1e30)
        local_top = jnp.max(cross_scores, axis=-1)
        global_top = taken_together(local_top, TOKENS)
        cross_exp = jnp.exp(cross_scores - global_top[..., None])
        local_total = jnp.sum(cross_exp, axis=-1)
        local_sum = jnp.einsum(
            "kgbs,skd->bkgd",
            cross_exp.astype(jnp.bfloat16),
            cache_values,
            preferred_element_type=jnp.float32,
        )
        summed, total = together((local_sum, local_total), (("tokens_0", "tokens_1"), "tokens_2"))
        cross_out = (
            (summed / total.transpose(2, 0, 1)[..., None])
            .astype(jnp.bfloat16)
            .reshape(beam_rows, head_local * DH)
        )
        branch = jnp.dot(
            cross_out, beam_out_weight[layer_index], preferred_element_type=jnp.float32
        )
        branch = over_copies(branch, "heads")
        state = (state_f + branch).astype(jnp.bfloat16)
    return (stretch_hidden, new_cache, state)


def solution(mesh):
    finer = Mesh(
        mesh.devices.reshape(mesh.shape["heads"], 4, 4, 2),
        ("heads", "tokens_0", "tokens_1", "tokens_2"),
    )
    placed = (
        P(TOKENS, "heads"),
        P(TOKENS, "heads"),
        P(TOKENS, None, "heads"),
        P("heads", TOKENS),
        P("heads"),
        P(None, None, "heads"),
        P(TOKENS, None, "heads"),
        P(),
        P(),
        P(None, TOKENS),
        P(),
        P(None, TOKENS),
        P(None, TOKENS, "heads"),
        P(None, "heads", TOKENS),
    )
    return jax.shard_map(
        shards,
        mesh=finer,
        in_specs=placed,
        out_specs=(P(TOKENS, "heads"), P(TOKENS, None, "heads"), P(None, TOKENS)),
        check_vma=False,
    )
```

profile of v0, /device:TPU:1, one launch (start us, length us, event | category | flops | bytes accessed | tf_op | source)
XLA Modules:
  0.0 538.4 jit_solution(10028710868636956972)
XLA Ops:
  8.9 4.6 collective-permute-start
  15.4 3.2 collective-permute-start.1
  19.8 3.2 collective-permute-done.1
  23.0 5.2 collective-permute-start.2
  29.2 11.0 %collective-permute-done.2 = bf16[1024,2,128]{2,0,1:T(8,128)(2,1)S(1)} collective-permute-done((bf16[1024,2,128]{2,0,1:T(8,128)(2,1)S(1)}, bf16[1024,2,128]{2,0,1:T(8,128)(2,1)S(1)}, u32[]{:S(2)}, u32[]{:S(2)}) %collective-permute-start.2) | collective-permute-done | bytes 524320 | tf_op jit(solution)/shard_map/ppermute | solution.py:21
  44.6 31.4 %all-gather.3.cloned.1.call-done = bf16[640,5120]{0,1:T(8,128)(2,1)} async-done(((bf16[640,160]{0,1:T(8,128)(2,1)}), bf16[640,5120]{0,1:T(8,128)(2,1)}) %all-gather.3.cloned.1.call-update) | async-done | bytes 6553616 | tf_op jit(solution)/shard_map/all_gather | solution.py:163
  76.0 7.5 %fusion.100 = f32[256,5120]{1,0:T(8,128)} fusion(bf16[256,640]{0,1:T(8,128)(2,1)S(1)} %bitcast.215, bf16[640,5120]{0,1:T(8,128)(2,1)} %all-gather.3.cloned.1.call-done), kind=kOutput, calls=%fused_computation.172 | convolution fusion | flops 1677721600 | bytes 12124160 | tf_op jit(solution)/shard_map/dot_general | solution.py:161
  83.7 63.7 %reduce-scatter.2.cloned.1.call-done = f32[256,640]{1,0:T(8,128)} async-done(((f32[256,5120]{1,0:T(8,128)}), f32[256,640]{1,0:T(8,128)}) %reduce-scatter.2.cloned.1.call-update) | async-done | bytes 655376 | tf_op jit(solution)/shard_map/reduce_scatter | solution.py:166
  152.2 7.6 %all-to-all-start.1 = ((f32[32,1,256]{2,1,0:T(1,128)}), f32[32,1,256]{2,1,0:T(1,128)S(1)}, u32[]{:S(2)}, u32[]{:S(2)}) async-start(f32[32,1,256]{2,1,0:T(1,128)} %broadcast_in_dim.120), calls=%async_computation.2 | async-start | bytes 65536 | tf_op jit(solution)/shard_map/all_to_all | solution.py:33
  159.8 7.3 %all-to-all-done.1 = f32[32,1,256]{2,1,0:T(1,128)S(1)} async-done(((f32[32,1,256]{2,1,0:T(1,128)}), f32[32,1,256]{2,1,0:T(1,128)S(1)}, u32[]{:S(2)}, u32[]{:S(2)}) %all-to-all-start.1) | async-done | bytes 32800 | tf_op jit(solution)/shard_map/all_to_all | solution.py:33
  167.6 4.3 all_to_all.133
  172.6 3.5 all-to-all-start.3
  176.2 8.5 %all-to-all-done.3 = f32[16,8,640]{2,1,0:T(8,128)S(1)} async-done(((f32[16,8,640]{2,1,0:T(8,128)}), f32[16,8,640]{2,1,0:T(8,128)S(1)}, u32[]{:S(2)}, u32[]{:S(2)}) %all-to-all-start.3) | async-done | bytes 327712 | tf_op jit(solution)/shard_map/all_to_all | solution.py:55
  185.5 3.8 all-to-all-start.4
  190.3 5.8 %all-to-all-done.4 = bf16[16,8,640]{2,1,0:T(8,128)(2,1)S(1)} async-done(((bf16[16,8,640]{2,1,0:T(8,128)(2,1)}), bf16[16,8,640]{2,1,0:T(8,128)(2,1)S(1)}, u32[]{:S(2)}, u32[]{:S(2)}) %all-to-all-start.4) | async-done | bytes 163872 | tf_op jit(solution)/shard_map/all_to_all | solution.py:33
  196.8 6.0 %all-to-all-start.5 = ((bf16[2,16,8,640]{3,2,1,0:T(8,128)(2,1)}), bf16[2,16,8,640]{3,2,1,0:T(8,128)(2,1)S(1)}, u32[]{:S(2)}, u32[]{:S(2)}) async-start(bf16[2,16,8,640]{3,2,1,0:T(8,128)(2,1)} %broadcast_in_dim.122), calls=%async_computation.6 | async-start | bytes 655360 | tf_op jit(solution)/shard_map/all_to_all | solution.py:33
  206.1 3.5 fusion.38
  212.1 15.9 %all-to-all-start = ((bf16[32,2,2048]{2,1,0:T(2,128)(2,1)}), bf16[32,2,2048]{2,1,0:T(2,128)(2,1)S(1)}, u32[]{:S(2)}, u32[]{:S(2)}) async-start(bf16[32,2,2048]{2,1,0:T(2,128)(2,1)} %reshape.444), calls=%async_computation.1 | async-start | bytes 524288 | tf_op jit(solution)/shard_map/all_to_all | solution.py:187
  228.9 3.3 reshape.413
  232.6 4.4 all-to-all-done
  240.1 3.2 reshape.414
  243.3 3.8 fusion.97
  247.2 9.6 %bitcast_reduce_fusion.1 = (f32[5,256]{1,0:T(8,128)S(1)}, f32[4096,256,5]{1,0,2:T(8,128)}) fusion(pred[4096]{0:T(1024)(128)(4,1)S(1)} %fusion.75, bf16[256,5,128]{2,1,0:T(8,128)(2,1)S(1)} %convert_element_type.189, bf16[4096,1,128]{2,1,0:T(2,128)(2,1)S(1)} %get-tuple-element.27), kind=kOutput, calls=%fused_computation.6 | convolution fusion | flops 1357904640 | bytes 22356992 | tf_op jit(solution)/shard_map/bkgd,skd->kgbs/dot_general | solution.py:232
  257.5 3.7 all-to-all-start.6
  261.2 4.7 copy.240
  265.9 3.4 all-to-all-done.6
  269.4 10.6 %fusion.2 = f32[5,256]{1,0:T(8,128)S(1)} fusion(f32[4096,256,5]{1,0,2:T(8,128)} %get-tuple-element.35, f32[5,256]{1,0:T(8,128)S(1)} %reduce_max.47, pred[4096]{0:T(1024)(128)(4,1)S(1)} %fusion.75), kind=kLoop, calls=%fused_computation.9 | loop fusion | flops 20970240 | bytes 20985856 | tf_op jit(solution)/shard_map/reduce_sum | solution.py:239
  282.4 5.1 fusion.32
  288.7 4.2 all_to_all.134
  293.3 11.5 %all_to_all.135 = f32[16,1,5160]{2,1,0:T(1,128)S(1)} all-to-all(f32[16,1,5160]{2,1,0:T(1,128)S(1)} %all_to_all.91), channel_id=1, replica_groups=mesh['heads'=8,'tokens_0'=4,'tokens_1'=4,'tokens_2'=2] {'tokens_0','toke..., dimensions={0} | all-to-all | bytes 660480 | tf_op jit(solution)/shard_map/all_to_all | solution.py:55
  305.1 11.6 %all_to_all.136 = f32[16,1,5160]{2,1,0:T(1,128)S(1)} all-to-all(f32[16,1,5160]{2,1,0:T(1,128)S(1)} %broadcast_in_dim.125), channel_id=1, replica_groups=mesh['heads'=8,'tokens_0'=4,'tokens_1'=4,'tokens_2'=2] {'tokens_0','toke..., dimensions={0} | all-to-all | bytes 660480 | tf_op jit(solution)/shard_map/all_to_all | solution.py:33
  316.9 6.8 %all_to_all.137 = f32[2,16,5160]{2,1,0:T(8,128)S(1)} all-to-all(f32[2,16,5160]{2,1,0:T(8,128)S(1)} %broadcast_in_dim.126), channel_id=1, replica_groups=mesh['heads'=8,'tokens_0'=4,'tokens_1'=4,'tokens_2'=2] {'tokens_2'}, dimensions={0} | all-to-all | bytes 1320960 | tf_op jit(solution)/shard_map/all_to_all | solution.py:33
  326.7 37.6 %all_to_all.138 = f32[8,256,160]{1,2,0:T(8,128)S(1)} all-to-all(f32[8,256,160]{1,2,0:T(8,128)S(1)} %broadcast_in_dim.127), channel_id=1, replica_groups=mesh['heads'=8,'tokens_0'=4,'tokens_1'=4,'tokens_2'=2] {'heads'}, dimensions={0} | all-to-all | bytes 2621440 | tf_op jit(solution)/shard_map/all_to_all | solution.py:33
  366.3 12.5 %all_to_all.139 = f32[32,1,256]{2,1,0:T(1,128)S(1)} all-to-all(f32[32,1,256]{2,1,0:T(1,128)S(1)} %broadcast_in_dim.128), channel_id=1, replica_groups=mesh['heads'=8,'tokens_0'=4,'tokens_1'=4,'tokens_2'=2] {'tokens_0','toke..., dimensions={0} | all-to-all | bytes 65536 | tf_op jit(solution)/shard_map/all_to_all | solution.py:33
  380.2 4.3 all_to_all.140
  384.6 10.7 %all_to_all.141 = f32[16,8,640]{2,1,0:T(8,128)S(1)} all-to-all(f32[16,8,640]{2,1,0:T(8,128)S(1)} %reduce_sum.184), channel_id=1, replica_groups=mesh['heads'=8,'tokens_0'=4,'tokens_1'=4,'tokens_2'=2] {'tokens_0','toke..., dimensions={0} | all-to-all | bytes 655360 | tf_op jit(solution)/shard_map/all_to_all | solution.py:55
  395.3 10.7 %all_to_all.142 = bf16[16,8,640]{2,1,0:T(8,128)(2,1)S(1)} all-to-all(bf16[16,8,640]{2,1,0:T(8,128)(2,1)S(1)} %broadcast_in_dim.129), channel_id=1, replica_groups=mesh['heads'=8,'tokens_0'=4,'tokens_1'=4,'tokens_2'=2] {'tokens_0','toke..., dimensions={0} | all-to-all | bytes 327680 | tf_op jit(solution)/shard_map/all_to_all | solution.py:33
  406.1 6.5 %all_to_all.143 = bf16[2,16,8,640]{3,2,1,0:T(8,128)(2,1)S(1)} all-to-all(bf16[2,16,8,640]{3,2,1,0:T(8,128)(2,1)S(1)} %broadcast_in_dim.130), channel_id=1, replica_groups=mesh['heads'=8,'tokens_0'=4,'tokens_1'=4,'tokens_2'=2] {'tokens_2'}, dimensions={0} | all-to-all | bytes 655360 | tf_op jit(solution)/shard_map/all_to_all | solution.py:33
  413.0 9.6 %bitcast_reduce_fusion = (f32[5,256]{1,0:T(8,128)S(1)}, f32[4096,256,5]{1,0,2:T(8,128)}) fusion(pred[4096]{0:T(1024)(128)(4,1)S(1)} %fusion.75, bf16[256,5,128]{2,1,0:T(8,128)(2,1)S(1)} %convert_element_type.198, bf16[4096,1,128]{2,1,0:T(2,128)(2,1)S(1)} %copy-done.4), kind=kOutput, calls=%fused_computation.2 | convolution fusion | flops 1357904640 | bytes 22356992 | tf_op jit(solution)/shard_map/bkgd,skd->kgbs/dot_general | solution.py:232
  422.7 11.9 %all_to_all.144 = f32[32,1,5,256]{3,1,2,0:T(1,128)S(1)} all-to-all(f32[32,1,5,256]{3,1,2,0:T(1,128)S(1)} %broadcast_in_dim.131), channel_id=1, replica_groups=mesh['heads'=8,'tokens_0'=4,'tokens_1'=4,'tokens_2'=2] {'tokens_0','toke..., dimensions={0} | all-to-all | bytes 327680 | tf_op jit(solution)/shard_map/all_to_all | solution.py:33
  434.6 10.1 %fusion.29 = f32[256,1,5,128]{0,3,2,1:T(8,128)S(1)} fusion(f32[4096,256,5]{1,0,2:T(8,128)} %get-tuple-element.37, f32[5,256]{1,0:T(8,128)S(1)} %reduce_max.49, pred[4096]{0:T(1024)(128)(4,1)S(1)} %fusion.75, bf16[4096,1,128]{0,2,1:T(8,128)(2,1)} %copy-done.6), kind=kOutput, calls=%fused_computation.43 | convolution fusion | flops 1363148800 | bytes 22684672 | tf_op jit(solution)/shard_map/kgbs,skd->bkgd/dot_general | solution.py:240
  444.7 3.2 copy-done.1
  447.9 5.6 %fusion.4 = f32[5,256]{1,0:T(8,128)S(1)} fusion(f32[4096,256,5]{1,0,2:T(8,128)S(1)} %copy-done.1, f32[5,256]{1,0:T(8,128)S(1)} %reduce_max.49, pred[4096]{0:T(1024)(128)(4,1)S(1)} %fusion.75), kind=kLoop, calls=%fused_computation.11 | loop fusion | flops 20970240 | bytes 20985856 | tf_op jit(solution)/shard_map/reduce_sum | solution.py:239
  454.8 4.2 all_to_all.145
  459.3 10.9 %all_to_all.146 = f32[16,1,5160]{2,1,0:T(1,128)S(1)} all-to-all(f32[16,1,5160]{2,1,0:T(1,128)S(1)} %all_to_all.104), channel_id=1, replica_groups=mesh['heads'=8,'tokens_0'=4,'tokens_1'=4,'tokens_2'=2] {'tokens_0','toke..., dimensions={0} | all-to-all | bytes 660480 | tf_op jit(solution)/shard_map/all_to_all | solution.py:55
  470.6 11.6 %all_to_all.147 = f32[16,1,5160]{2,1,0:T(1,128)S(1)} all-to-all(f32[16,1,5160]{2,1,0:T(1,128)S(1)} %broadcast_in_dim.132), channel_id=1, replica_groups=mesh['heads'=8,'tokens_0'=4,'tokens_1'=4,'tokens_2'=2] {'tokens_0','toke..., dimensions={0} | all-to-all | bytes 660480 | tf_op jit(solution)/shard_map/all_to_all | solution.py:33
  482.3 7.0 %all_to_all.148 = f32[2,16,5160]{2,1,0:T(8,128)S(1)} all-to-all(f32[2,16,5160]{2,1,0:T(8,128)S(1)} %broadcast_in_dim.133), channel_id=1, replica_groups=mesh['heads'=8,'tokens_0'=4,'tokens_1'=4,'tokens_2'=2] {'tokens_2'}, dimensions={0} | all-to-all | bytes 1320960 | tf_op jit(solution)/shard_map/all_to_all | solution.py:33
  493.2 37.2 %all_to_all.149 = f32[8,256,160]{1,2,0:T(8,128)S(1)} all-to-all(f32[8,256,160]{1,2,0:T(8,128)S(1)} %broadcast_in_dim.134), channel_id=1, replica_groups=mesh['heads'=8,'tokens_0'=4,'tokens_1'=4,'tokens_2'=2] {'heads'}, dimensions={0} | all-to-all | bytes 2621440 | tf_op jit(solution)/shard_map/all_to_all | solution.py:33
  (157 shorter events, 47.2 us)
Async XLA Ops:
  7.2 68.8 %all-gather.3.cloned.1.call-start = ((), (), s32[]{:S(2)}) async-start(), calls=%async_computation.24 | async-start | bytes 6758400 | tf_op jit(solution)/shard_map/all_gather | solution.py:163
  7.9 139.5 %reduce-scatter.2.cloned.1.call-start = ((), (), s32[]{:S(2)}) async-start(), calls=%async_computation.25 | async-start | bytes 5898240 | tf_op jit(solution)/shard_map/reduce_scatter | solution.py:166
  8.9 6.5 %collective-permute-start = (bf16[256,2,128]{2,0,1:T(8,128)(2,1)S(1)}, bf16[256,2,128]{2,0,1:T(8,128)(2,1)S(1)}, u32[]{:S(2)}, u32[]{:S(2)}) collective-permute-start(bf16[256,2,128]{2,0,1:T(8,128)(2,1)S(1)} %copy.190), channel_id=1, source_target_pairs={{0,1},{1,2},{2,3},{3,4},{4,5},{5,6},{6,7},{7,8},{8,9},{9,10},{10,1... | collective-permute-start | bytes 393224 | tf_op jit(solution)/shard_map/ppermute | solution.py:21
  15.4 7.6 %collective-permute-start.1 = (bf16[512,2,128]{2,0,1:T(8,128)(2,1)S(1)}, bf16[512,2,128]{2,0,1:T(8,128)(2,1)S(1)}, u32[]{:S(2)}, u32[]{:S(2)}) collective-permute-start(bf16[512,2,128]{2,0,1:T(8,128)(2,1)S(1)} %pad_maximum_fusion.4), channel_id=1, source_target_pairs={{0,2},{1,3},{2,4},{3,5},{4,6},{5,7},{6,8},{7,9},{8,10},{9,11},{10,... | collective-permute-start | bytes 786440 | tf_op jit(solution)/shard_map/ppermute | solution.py:21
  23.0 17.1 %collective-permute-start.2 = (bf16[1024,2,128]{2,0,1:T(8,128)(2,1)S(1)}, bf16[1024,2,128]{2,0,1:T(8,128)(2,1)S(1)}, u32[]{:S(2)}, u32[]{:S(2)}) collective-permute-start(bf16[1024,2,128]{2,0,1:T(8,128)(2,1)S(1)} %pad_maximum_fusion.2), channel_id=1, source_target_pairs={{0,4},{1,5},{2,6},{3,7},{4,8},{5,9},{6,10},{7,11},{8,12},{9,13},{1... | collective-permute-start | bytes 1572872 | tf_op jit(solution)/shard_map/ppermute | solution.py:21
  76.0 7.6 %copy-start.12 = (bf16[640]{0:T(1024)(128)(2,1)S(1)}, bf16[640]{0:T(1024)(128)(2,1)}, u32[]{:S(2)}) copy-start(bf16[640]{0:T(1024)(128)(2,1)} %param.18) | copy-start | bytes 3844
  76.0 71.4 %copy-start.9 = (bf16[256,640]{1,0:T(8,128)(2,1)S(1)}, bf16[256,640]{1,0:T(8,128)(2,1)}, u32[]{:S(2)}) copy-start(bf16[256,640]{1,0:T(8,128)(2,1)} %param.14) | copy-start | bytes 983044
  83.5 66.5 %copy-start.10 = (bf16[256,160]{0,1:T(8,128)(2,1)S(1)}, bf16[256,160]{0,1:T(8,128)(2,1)}, u32[]{:S(2)}) copy-start(bf16[256,160]{0,1:T(8,128)(2,1)} %param.23) | copy-start | bytes 245764
  83.5 66.6 %copy-start.14 = (s32[256]{0:T(256)S(1)}, s32[256]{0:T(256)}, u32[]{:S(2)}) copy-start(s32[256]{0:T(256)} %param.24) | copy-start | bytes 3076
  83.5 76.3 %copy-start.11 = (bf16[2,160]{1,0:T(2,128)(2,1)S(1)}, bf16[2,160]{1,0:T(2,128)(2,1)}, u32[]{:S(2)}) copy-start(bf16[2,160]{1,0:T(2,128)(2,1)} %param.25) | copy-start | bytes 1924
  83.5 83.7 %copy-start.8 = (bf16[2,160,640]{2,1,0:T(8,128)(2,1)S(1)}, bf16[2,160,640]{2,1,0:T(8,128)(2,1)}, u32[]{:S(2)}) copy-start(bf16[2,160,640]{2,1,0:T(8,128)(2,1)} %param.26) | copy-start | bytes 1228804
  83.5 92.7 %copy-start.13 = (s32[512]{0:T(512)S(1)}, s32[512]{0:T(512)}, u32[]{:S(2)}) copy-start(s32[512]{0:T(512)} %param.21) | copy-start | bytes 6148
  83.6 119.2 %all-gather.5.cloned.1.call-start = ((), (), s32[]{:S(2)}) async-start(), calls=%async_computation.26 | async-start | bytes 3041280 | tf_op jit(solution)/shard_map/all_gather | solution.py:27
  148.5 0.7 copy-start.5
  152.2 14.9 %all-to-all-start.1 = ((f32[32,1,256]{2,1,0:T(1,128)}), f32[32,1,256]{2,1,0:T(1,128)S(1)}, u32[]{:S(2)}, u32[]{:S(2)}) async-start(f32[32,1,256]{2,1,0:T(1,128)} %broadcast_in_dim.120), calls=%async_computation.2 | async-start | bytes 65536 | tf_op jit(solution)/shard_map/all_to_all | solution.py:33
  172.6 12.1 %all-to-all-start.3 = ((f32[16,8,640]{2,1,0:T(8,128)}), f32[16,8,640]{2,1,0:T(8,128)S(1)}, u32[]{:S(2)}, u32[]{:S(2)}) async-start(f32[16,8,640]{2,1,0:T(8,128)} %reduce_sum.176), calls=%async_computation.4 | async-start | bytes 655360 | tf_op jit(solution)/shard_map/all_to_all | solution.py:55
  185.5 10.6 %all-to-all-start.4 = ((bf16[16,8,640]{2,1,0:T(8,128)(2,1)}), bf16[16,8,640]{2,1,0:T(8,128)(2,1)S(1)}, u32[]{:S(2)}, u32[]{:S(2)}) async-start(bf16[16,8,640]{2,1,0:T(8,128)(2,1)} %broadcast_in_dim.121), calls=%async_computation.5 | async-start | bytes 327680 | tf_op jit(solution)/shard_map/all_to_all | solution.py:33
  196.8 15.3 %all-to-all-start.5 = ((bf16[2,16,8,640]{3,2,1,0:T(8,128)(2,1)}), bf16[2,16,8,640]{3,2,1,0:T(8,128)(2,1)S(1)}, u32[]{:S(2)}, u32[]{:S(2)}) async-start(bf16[2,16,8,640]{3,2,1,0:T(8,128)(2,1)} %broadcast_in_dim.122), calls=%async_computation.6 | async-start | bytes 655360 | tf_op jit(solution)/shard_map/all_to_all | solution.py:33
  212.1 24.9 %all-to-all-start = ((bf16[32,2,2048]{2,1,0:T(2,128)(2,1)}), bf16[32,2,2048]{2,1,0:T(2,128)(2,1)S(1)}, u32[]{:S(2)}, u32[]{:S(2)}) async-start(bf16[32,2,2048]{2,1,0:T(2,128)(2,1)} %reshape.444), calls=%async_computation.1 | async-start | bytes 524288 | tf_op jit(solution)/shard_map/all_to_all | solution.py:187
  243.3 13.4 %copy-start.2 = (bf16[4096,2,128]{2,1,0:T(2,128)(2,1)}, bf16[4096,2,128]{2,1,0:T(2,128)(2,1)S(1)}, u32[]{:S(2)}) copy-start(bf16[4096,2,128]{2,1,0:T(2,128)(2,1)S(1)} %reshape.414) | copy-start | bytes 6291460
  247.2 9.6 %copy-start.3 = (bf16[4096,1,128]{2,1,0:T(2,128)(2,1)}, bf16[4096,1,128]{2,1,0:T(2,128)(2,1)S(1)}, u32[]{:S(2)}) copy-start(bf16[4096,1,128]{2,1,0:T(2,128)(2,1)S(1)} %get-tuple-element.27) | copy-start | bytes 3145732
  257.5 11.8 %all-to-all-start.6 = ((f32[32,1,5,256]{3,1,2,0:T(1,128)}), f32[32,1,5,256]{3,1,2,0:T(1,128)S(1)}, u32[]{:S(2)}, u32[]{:S(2)}) async-start(f32[32,1,5,256]{3,1,2,0:T(1,128)} %broadcast_in_dim.124), calls=%async_computation.7 | async-start | bytes 327680 | tf_op jit(solution)/shard_map/all_to_all | solution.py:33
  265.9 14.1 %copy-start.6 = (bf16[4096,1,128]{0,2,1:T(8,128)(2,1)}, bf16[4096,1,128]{0,2,1:T(8,128)(2,1)S(1)}, u32[]{:S(2)}) copy-start(bf16[4096,1,128]{0,2,1:T(8,128)(2,1)S(1)} %copy.240) | copy-start | bytes 3145732
  269.4 13.0 %copy-start = (f32[4096,256,5]{1,0,2:T(8,128)S(1)}, f32[4096,256,5]{1,0,2:T(8,128)}, u32[]{:S(2)}) copy-start(f32[4096,256,5]{1,0,2:T(8,128)} %get-tuple-element.35) | copy-start | bytes 62914564
  293.0 33.3 %copy-start.7 = (bf16[2,640,160]{1,2,0:T(8,128)(2,1)S(1)}, bf16[2,640,160]{1,2,0:T(8,128)(2,1)}, u32[]{:S(2)}) copy-start(bf16[2,640,160]{1,2,0:T(8,128)(2,1)} %param.27) | copy-start | bytes 1228804
  326.7 86.3 %copy-start.4 = (bf16[4096,1,128]{2,1,0:T(2,128)(2,1)S(1)}, bf16[4096,1,128]{2,1,0:T(2,128)(2,1)}, u32[]{:S(2)}) copy-start(bf16[4096,1,128]{2,1,0:T(2,128)(2,1)} %copy-done.3) | copy-start | bytes 3145732
  434.6 13.2 %copy-start.1 = (f32[4096,256,5]{1,0,2:T(8,128)S(1)}, f32[4096,256,5]{1,0,2:T(8,128)}, u32[]{:S(2)}) copy-start(f32[4096,256,5]{1,0,2:T(8,128)} %get-tuple-element.37) | copy-start | bytes 62914564
Sparse Core Ops, SparseCore 0:
  10.5 65.4 all-gather.2
  83.7 63.6 reduce-scatter.1
  150.1 38.6 all-gather.4
where the time goes:
time: 548 us; the launch traced here: 538 us
  blocking collectives  204 us (37%)
  waiting for transfers between devices  141 us (26%)
  matrix products  54.6 us (10%)
  starting transfers between devices  53.6 us (10%)
  local copies, waits for them, and re-layouts  41.5 us (8%)
  other arithmetic  28.2 us (5%)
  between operations  15.7 us (3%)
    all_to_all x10, blocking collectives, copy_for_each(): return lax.all_to_all(copies, axis, split_axis=0, concat_axis=0, tiled=True)  154 us
    reduce_scatter x1, waiting for transfers between devices, shards(): lax.psum_scatter(partial_out, 'heads', scatter_dimension=1, tiled=True)  63.7 us
    all_to_all x3, blocking collectives, sum_in_two_steps(): return jnp.sum(lax.all_to_all(own, far, 0, 0, tiled=True), axis=0)  33 us
    all_gather x1, waiting for transfers between devices, shards(): lax.all_gather(out_weight, TOKENS, axis=1, tiled=True)  31.4 us
    all_to_all x4, starting transfers between devices, copy_for_each(): return lax.all_to_all(copies, axis, split_axis=0, concat_axis=0, tiled=True)  21.1 us
    dot_general x2, matrix products, shards(): jnp.einsum('bkgd,skd->kgbs', query_rows, cache_keys, preferred_element_ty...  19.2 us
    all_to_all x4, blocking collectives, sent_and_summed(): lax.all_to_all(parts, axis, split_axis=0, concat_axis=0, tiled=True)  17 us
    all_to_all x4, waiting for transfers between devices, copy_for_each(): return lax.all_to_all(copies, axis, split_axis=0, concat_axis=0, tiled=True)  16.4 us
  transfers between devices with their start and end apart: 12, of which 10 were waited for; matrix products, arithmetic and copies ran while one was open for 6% of the time, Pallas kernels for 0%

commit v1 on v0

v1 whole, which is shorter than its diff:
```python
import functools
import math

import jax
import jax.numpy as jnp
from jax import lax
from jax.experimental import pallas as pl
from jax.experimental.pallas import tpu as pltpu
from jax.sharding import PartitionSpec as P

D = 5120
DH = 128
WINDOW = 1024
PAGE = 16
LAYERS = 2
EPSILON = 1e-06
SCALE = DH ** (-0.5)
SCALE2 = SCALE * math.log2(math.e)
MESH = pl.DeviceIdType.MESH
VMEM_SPEC = pl.BlockSpec(memory_space=pltpu.VMEM)


def scatter_start(send, recv, sems, axis, count, me):
    def one(step, carry):
        peer = lax.rem(me + step, count)
        pltpu.make_async_remote_copy(
            src_ref=send.at[peer],
            dst_ref=recv.at[me],
            send_sem=sems.at[0],
            recv_sem=sems.at[1],
            device_id={axis: peer},
            device_id_type=MESH,
        ).start()
        return carry

    lax.fori_loop(1, count, one, 0)


def gather_start(held, sems, axis, count, me):
    def one(step, carry):
        peer = lax.rem(me + step, count)
        pltpu.make_async_remote_copy(
            src_ref=held.at[me],
            dst_ref=held.at[me],
            send_sem=sems.at[0],
            recv_sem=sems.at[1],
            device_id={axis: peer},
            device_id_type=MESH,
        ).start()
        return carry

    lax.fori_loop(1, count, one, 0)


def finish(held, sems, axis, count, me):
    everything = held.at[pl.ds(0, count - 1)]
    pltpu.make_async_remote_copy(
        src_ref=everything,
        dst_ref=everything,
        send_sem=sems.at[0],
        recv_sem=sems.at[1],
        device_id={axis: lax.rem(me + 1, count)},
        device_id_type=MESH,
    ).wait()


def greet(axis, count, me):
    barrier = pltpu.get_barrier_semaphore()

    def one(step, carry):
        pl.semaphore_signal(
            barrier, inc=1, device_id={axis: lax.rem(me + step, count)}, device_id_type=MESH
        )
        return carry

    lax.fori_loop(1, count, one, 0)


def beam_kernel(do_out, do_query, do_pages, n_tok, n_head, *refs):
    refs = list(refs)
    take = lambda k: [refs.pop(0) for _ in range(k)]
    if do_out:
        o_ref, lse_ref, wo_ref = take(3)
    (state_ref,) = take(1)
    if do_query:
        gain_ref, wq_ref = take(2)
    if do_pages:
        (outbox_ref,) = take(1)
    if do_out:
        (state_out_ref,) = take(1)
    if do_query:
        (q_out_ref,) = take(1)
    if do_pages:
        (inbox_out_ref,) = take(1)
    if do_out:
        o_recv, lse_recv, o_held, b_send, b_recv, s_held = take(6)
    if do_query:
        q_send, q_recv, q_held = take(3)
    if do_pages:
        (inbox,) = take(1)
    (sems,) = take(1)

    me_t = lax.axis_index("tokens")
    me_h = lax.axis_index("heads")
    tok = ("tokens", n_tok, me_t)
    head = ("heads", n_head, me_h)
    greet(*tok)
    peers = n_tok - 1
    if do_out:
        greet(*head)
        peers += n_head - 1
    pl.semaphore_wait(pltpu.get_barrier_semaphore(), peers)

    if do_out:
        scatter_start(o_ref, o_recv, sems.at[0], *tok)
        scatter_start(lse_ref, lse_recv, sems.at[1], *tok)
    if do_pages:
        scatter_start(outbox_ref, inbox, sems.at[2], *tok)
        inbox[me_t] = outbox_ref[me_t]
    if do_out:
        o_recv[me_t] = o_ref[me_t]
        lse_recv[me_t] = lse_ref[me_t]
        finish(lse_recv, sems.at[1], *tok)
        lse = lse_recv[...]
        weight = jnp.exp2(lse - jnp.max(lse, axis=0, keepdims=True))
        share = weight / jnp.sum(weight, axis=0, keepdims=True)
        finish(o_recv, sems.at[0], *tok)
        for g in range(o_ref.shape[2] // DH):
            cols = slice(g * DH, (g + 1) * DH)
            mixed = jnp.sum(o_recv[:, :, cols].astype(jnp.float32) * share[:, :, g : g + 1], axis=0)
            o_held[me_t, :, cols] = mixed.astype(jnp.bfloat16)
        gather_start(o_held, sems.at[3], *tok)
        finish(o_held, sems.at[3], *tok)
        width = o_ref.shape[2]
        whole = o_held[...].astype(jnp.float32).reshape(-1, width).astype(jnp.bfloat16)
        branch = jnp.dot(whole, wo_ref[...], preferred_element_type=jnp.float32)
        b_send[...] = branch.reshape(b_send.shape).astype(jnp.bfloat16)
        scatter_start(b_send, b_recv, sems.at[4], *head)
        b_recv[me_h] = b_send[me_h]
        finish(b_recv, sems.at[4], *head)
        total = jnp.sum(b_recv[...].astype(jnp.float32), axis=0)
        s_held[me_h] = (state_ref[me_h].astype(jnp.float32) + total).astype(jnp.bfloat16)
        gather_start(s_held, sems.at[5], *head)
        finish(s_held, sems.at[5], *head)
        state_out_ref[...] = s_held[...]
        state = s_held[...]
    else:
        state = state_ref[...]
    if do_query:
        state = state.astype(jnp.float32).reshape(-1, state.shape[2])
        squares = jnp.sum(state * state, axis=1, keepdims=True)
        scaled = (state * gain_ref[...].astype(jnp.float32)).astype(jnp.bfloat16)
        part = jnp.dot(scaled, wq_ref[...], preferred_element_type=jnp.float32)
        width = part.shape[1]
        rows = part.shape[0] // n_tok
        q_send[:, :, :width] = part.reshape(n_tok, rows, width).astype(jnp.bfloat16)
        q_send[:, :, width:] = (
            jnp.broadcast_to(squares, (part.shape[0], DH))
            .reshape(n_tok, rows, DH)
            .astype(jnp.bfloat16)
        )
        scatter_start(q_send, q_recv, sems.at[6], *tok)
        q_recv[me_t] = q_send[me_t]
        finish(q_recv, sems.at[6], *tok)
        total = jnp.sum(q_recv[...].astype(jnp.float32), axis=0)
        factor = lax.rsqrt(total[:, width : width + 1] / D + EPSILON)
        q_held[me_t] = (total[:, :width] * factor).astype(jnp.bfloat16)
        gather_start(q_held, sems.at[7], *tok)
        finish(q_held, sems.at[7], *tok)
        q_out_ref[...] = q_held[...].astype(jnp.float32).reshape(-1, width).astype(jnp.bfloat16)
    if do_pages:
        finish(inbox, sems.at[2], *tok)
        inbox_out_ref[...] = inbox[...]


def beam_step(n_tok, n_head, collective_id, state, out=None, query=None, pages=None):
    do_out, do_query, do_pages = (out is not None, query is not None, pages is not None)
    beams, cols = state.shape
    state3 = state.reshape(n_head, beams // n_head, cols)
    bf16 = jnp.bfloat16
    args, out_shape, scratch = [], [], []
    if do_out:
        o, lse, wo = out
        width = o.shape[1]
        args += [o.reshape(n_tok, -1, width), lse.reshape(n_tok, -1, DH), wo]
        out_shape += [jax.ShapeDtypeStruct(state3.shape, bf16)]
        rows = beams // n_tok
        scratch += [
            pltpu.VMEM((n_tok, rows, width), bf16),
            pltpu.VMEM((n_tok, rows, DH), jnp.float32),
            pltpu.VMEM((n_tok, rows, width), bf16),
            pltpu.VMEM(state3.shape, bf16),
            pltpu.VMEM(state3.shape, bf16),
            pltpu.VMEM(state3.shape, bf16),
        ]
    args += [state3]
    if do_query:
        gain, wq = query
        args += [gain, wq]
        width = wq.shape[1]
        out_shape += [jax.ShapeDtypeStruct((beams, width), bf16)]
        rows = beams // n_tok
        scratch += [
            pltpu.VMEM((n_tok, rows, width + DH), bf16),
            pltpu.VMEM((n_tok, rows, width + DH), bf16),
            pltpu.VMEM((n_tok, rows, width), bf16),
        ]
    if do_pages:
        args += [pages]
        out_shape += [jax.ShapeDtypeStruct(pages.shape, bf16)]
        scratch += [pltpu.VMEM(pages.shape, bf16)]
    scratch += [pltpu.SemaphoreType.DMA((8, 2))]
    res = pl.pallas_call(
        functools.partial(beam_kernel, do_out, do_query, do_pages, n_tok, n_head),
        out_shape=out_shape,
        in_specs=[VMEM_SPEC] * len(args),
        out_specs=[VMEM_SPEC] * len(out_shape),
        scratch_shapes=scratch,
        compiler_params=pltpu.CompilerParams(
            collective_id=collective_id, has_side_effects=True, vmem_limit_bytes=32 << 20
        ),
        name=f"beam_step_{collective_id}",
    )(*args)
    res = list(res)
    if do_out:
        res[0] = res[0].reshape(beams, cols)
    return res


def attend_kernel(blocks, block, has_fresh, has_carry, last, *refs):
    refs = list(refs)
    q_ref = refs.pop(0)
    if blocks:
        k_ref, v_ref, bias_ref = [refs.pop(0) for _ in range(3)]
    if has_fresh:
        kf_ref, vf_ref = [refs.pop(0) for _ in range(2)]
    if has_carry:
        acc_in_ref, top_in_ref = [refs.pop(0) for _ in range(2)]
    if last:
        o_ref, lse_ref, acc, top = refs
    else:
        acc, top = refs
    g = pl.program_id(0)
    q = q_ref[...]
    rows = q.shape[0]
    if has_carry:
        acc[...] = acc_in_ref[...]
        top[...] = top_in_ref[...]
    else:
        acc[...] = jnp.zeros(acc.shape, jnp.float32)
        top[...] = jnp.full(top.shape, -1e30, jnp.float32)

    def step(keys, values, bias):
        s = lax.dot_general(
            q, keys, (((1,), (1,)), ((), ())), preferred_element_type=jnp.float32
        )
        if bias is not None:
            s = s + bias
        before = top[...]
        here = jnp.maximum(before, jnp.max(s, axis=1, keepdims=True))
        p = jnp.exp2((s - here[:, :1]) * SCALE2).astype(jnp.bfloat16)
        shrink = jnp.exp2((before - here) * SCALE2)
        top[...] = here
        pv = jnp.dot(p, values, preferred_element_type=jnp.float32)
        acc[...] = acc[...] * jnp.concatenate([shrink, shrink], axis=1) + pv

    if blocks:

        def body(b, carry):
            at = pl.ds(pl.multiple_of(b * block, block), block)
            step(k_ref[at, :], v_ref[at, :], bias_ref[:, at])
            return carry

        lax.fori_loop(0, blocks, body, 0)
    if has_fresh:
        step(kf_ref[...], vf_ref[...], None)
    if last:
        amount = acc[:, DH:]
        o_ref[...] = (acc[:, :DH] / amount).astype(jnp.bfloat16)
        lane = lax.broadcasted_iota(jnp.int32, (rows, DH), 1)
        value = top[...] * SCALE2 + jnp.log2(amount)
        kept = jnp.where(g == 0, jnp.zeros_like(value), lse_ref[...])
        lse_ref[...] = jnp.where(lane == g, value, kept)


def attend(q, old=None, fresh=None, carry=None, block=1024):
    beams, width = q.shape
    groups = width // DH
    args, specs = [q], [pl.BlockSpec((beams, DH), lambda g: (0, g))]
    whole = lambda a: pl.BlockSpec(a.shape, lambda g: (0,) * a.ndim)
    blocks = 0
    for extra in (old, fresh):
        if extra is not None:
            args += list(extra)
            specs += [whole(a) for a in extra]
    if old is not None:
        blocks = old[0].shape[0] // block
    last = fresh is not None
    acc_spec = pl.BlockSpec((beams, 2 * DH), lambda g: (0, g))
    top_spec = pl.BlockSpec((beams, DH), lambda g: (0, g))
    if carry is not None:
        args += list(carry)
        specs += [acc_spec, top_spec]
    if last:
        out_shape = [
            jax.ShapeDtypeStruct((beams, width), jnp.bfloat16),
            jax.ShapeDtypeStruct((beams, DH), jnp.float32),
        ]
        out_specs = [
            pl.BlockSpec((beams, DH), lambda g: (0, g)),
            pl.BlockSpec((beams, DH), lambda g: (0, 0)),
        ]
        scratch = [
            pltpu.VMEM((beams, 2 * DH), jnp.float32),
            pltpu.VMEM((beams, DH), jnp.float32),
        ]
    else:
        out_shape = [
            jax.ShapeDtypeStruct((beams, 2 * width), jnp.float32),
            jax.ShapeDtypeStruct((beams, width), jnp.float32),
        ]
        out_specs = [acc_spec, top_spec]
        scratch = []
    rows = sum(a[0].shape[0] for a in (old, fresh) if a is not None)
    return pl.pallas_call(
        functools.partial(
            attend_kernel, blocks, block, fresh is not None, carry is not None, last
        ),
        grid=(groups,),
        out_shape=out_shape,
        in_specs=specs,
        out_specs=out_specs,
        scratch_shapes=scratch,
        compiler_params=pltpu.CompilerParams(vmem_limit_bytes=40 << 20),
        cost_estimate=pl.CostEstimate(
            flops=4 * beams * width * rows,
            bytes_accessed=rows * 3 * DH * 2,
            transcendentals=beams * groups * rows,
        ),
        name=f"attend_{blocks}_{int(last)}",
    )(*args)


def place_kernel(page_rows, slots, row_ref, cache_ref, inbox_ref, out_ref, sem):
    def copy(slot):
        return pltpu.make_async_copy(
            inbox_ref.at[slot], out_ref.at[pl.ds(row_ref[slot] * page_rows, page_rows)], sem
        )

    def start(slot, carry):
        @pl.when(row_ref[slot] >= 0)
        def _():
            copy(slot).start()

        return carry

    def wait(slot, carry):
        @pl.when(row_ref[slot] >= 0)
        def _():
            copy(slot).wait()

        return carry

    lax.fori_loop(0, slots, start, 0)
    lax.fori_loop(0, slots, wait, 0)


def place_pages(rows, cache, inbox):
    return pl.pallas_call(
        functools.partial(place_kernel, PAGE, inbox.shape[0]),
        out_shape=jax.ShapeDtypeStruct(cache.shape, cache.dtype),
        in_specs=[
            pl.BlockSpec(memory_space=pltpu.SMEM),
            pl.BlockSpec(memory_space=pl.ANY),
            pl.BlockSpec(memory_space=pl.ANY),
        ],
        out_specs=pl.BlockSpec(memory_space=pl.ANY),
        scratch_shapes=[pltpu.SemaphoreType.DMA],
        input_output_aliases={1: 0},
        name="place_pages",
    )(rows, cache, inbox)


def shards(
    hidden_in,
    queries,
    keyvals,
    out_weight,
    kv_gain,
    kv_weight,
    cache,
    page_home,
    cache_len,
    beam_state,
    parents,
    beam_gain,
    query_weight,
    beam_out_weight,
):
    n_tok = lax.axis_size("tokens")
    n_head = lax.axis_size("heads")
    tok_rows = hidden_in.shape[0]
    head_local = queries.shape[1] // DH
    me = lax.axis_index("tokens")
    reach_back = -(-WINDOW // tok_rows)

    state = jnp.take(beam_state, parents, axis=0)
    (q,) = beam_step(n_tok, n_head, 1, state, query=(beam_gain[0:1], query_weight[0]))

    cache_rows = cache.shape[0]
    pages_here = cache_rows // PAGE
    local_page = jnp.where(page_home // pages_here == me, page_home % pages_here, -1)
    page_ids = jnp.arange(pages_here, dtype=jnp.int32)
    written = jnp.any(page_ids[:, None] == local_page[None, :], axis=1)
    row_ids = me * cache_rows + jnp.arange(cache_rows, dtype=jnp.int32)
    kept = (row_ids < cache_len[0]) & ~jnp.repeat(written, PAGE)
    bias = jnp.where(kept, 0.0, -1e30).astype(jnp.float32)[None, :]
    old_keys = cache[:, 0]
    old_values = jnp.concatenate([cache[:, 1], jnp.ones_like(old_keys)], axis=1)
    old = (old_keys, old_values, bias)
    carry = attend(q, old=old)

    blocks = [keyvals]
    for back in range(1, reach_back + 1):
        pairs = [(s, s + back) for s in range(n_tok - back)]
        blocks.insert(0, lax.ppermute(keyvals, "tokens", pairs))
    window_rows = jnp.concatenate(blocks, axis=0)
    query_block = queries.reshape(tok_rows, head_local, DH)
    scores = (
        jnp.einsum(
            "tgd,sd->gts", query_block, window_rows[:, 0], preferred_element_type=jnp.float32
        )
        * SCALE
    )
    query_pos = me * tok_rows + jnp.arange(tok_rows, dtype=jnp.int32)
    key_pos = (me - reach_back) * tok_rows + jnp.arange(window_rows.shape[0], dtype=jnp.int32)
    allowed = (
        (key_pos[None, :] <= query_pos[:, None])
        & (key_pos[None, :] > query_pos[:, None] - WINDOW)
        & (key_pos[None, :] >= 0)
    )
    scores = jnp.where(allowed, scores, -1e30)
    expo = jnp.exp(scores - jnp.max(scores, axis=-1, keepdims=True))
    weights = (expo / jnp.sum(expo, axis=-1, keepdims=True)).astype(jnp.bfloat16)
    attended = jnp.einsum(
        "gts,sd->tgd", weights, window_rows[:, 1], preferred_element_type=jnp.float32
    )
    attended = attended.astype(jnp.bfloat16).reshape(tok_rows, head_local * DH)

    partial_out = jnp.dot(
        attended,
        lax.all_gather(out_weight, "tokens", axis=1, tiled=True),
        preferred_element_type=jnp.float32,
    ).astype(jnp.bfloat16)
    head_total = lax.psum_scatter(partial_out, "heads", scatter_dimension=1, tiled=True)
    stretch_hidden = (
        hidden_in.astype(jnp.float32) + head_total.astype(jnp.float32)
    ).astype(jnp.bfloat16)
    both = jnp.concatenate([stretch_hidden, jnp.tile(kv_gain[None, :], (16, 1))], axis=0)
    both = lax.all_gather(both, "heads", axis=1, tiled=True)
    hidden_f = both[:tok_rows].astype(jnp.float32)
    gain_f = both[tok_rows].astype(jnp.float32)
    factor = lax.rsqrt(jnp.mean(hidden_f * hidden_f, axis=1) + EPSILON)
    full_rows = (hidden_f * factor[:, None] * gain_f).astype(jnp.bfloat16)
    fresh = jnp.dot(
        full_rows, kv_weight.reshape(kv_weight.shape[0], -1), preferred_element_type=jnp.float32
    ).astype(jnp.bfloat16)

    own_pages = tok_rows // PAGE
    pages = fresh.reshape(own_pages, PAGE, -1)
    shift = page_home[0] // pages_here
    empty = jnp.zeros((n_tok - own_pages, *pages.shape[1:]), pages.dtype)
    ring = jnp.concatenate([pages, empty, pages, empty], axis=0)
    begin = (2 * n_tok * own_pages - shift - own_pages * me) % n_tok
    outbox = lax.dynamic_slice_in_dim(ring, begin, n_tok, 0)
    source = jnp.arange(n_tok, dtype=jnp.int32)
    which = (me - shift - own_pages * source + 2 * n_tok * own_pages) % n_tok
    landing = jnp.where(
        which < own_pages,
        jnp.take(page_home, jnp.minimum(own_pages * source + which, page_home.shape[0] - 1))
        % pages_here,
        -1,
    )

    fresh_keys = fresh[:, :DH]
    fresh_values = jnp.concatenate([fresh[:, DH:], jnp.ones_like(fresh_keys)], axis=1)
    new = (fresh_keys, fresh_values)
    o, lse = attend(q, fresh=new, carry=carry)
    state, q, inbox = beam_step(
        n_tok,
        n_head,
        2,
        state,
        out=(o, lse, beam_out_weight[0]),
        query=(beam_gain[1:2], query_weight[1]),
        pages=outbox,
    )
    new_cache = place_pages(landing, cache, inbox.reshape(n_tok, PAGE, *cache.shape[1:]))
    o, lse = attend(q, old=old, fresh=new)
    (state,) = beam_step(n_tok, n_head, 3, state, out=(o, lse, beam_out_weight[1]))
    return (stretch_hidden, new_cache, state)


def solution(mesh):
    tokens = "tokens"
    placed = (
        P(tokens, "heads"),
        P(tokens, "heads"),
        P(tokens, None, "heads"),
        P("heads", tokens),
        P("heads"),
        P(None, None, "heads"),
        P(tokens, None, "heads"),
        P(),
        P(),
        P(None, tokens),
        P(),
        P(None, tokens),
        P(None, tokens, "heads"),
        P(None, "heads", tokens),
    )
    return jax.shard_map(
        shards,
        mesh=mesh,
        in_specs=placed,
        out_specs=(P(tokens, "heads"), P(tokens, None, "heads"), P(None, tokens)),
        check_vma=False,
    )
```

time: 548 us -> 311 us (0.57); the launches traced: 538 us -> 310 us
  blocking collectives: 204 us -> 0 us
  Pallas kernels: 0 us -> 154 us
  waiting for transfers between devices: 141 us -> 71.5 us
  starting transfers between devices: 53.6 us -> 15.5 us
  matrix products: 54.6 us -> 17.5 us
  other arithmetic: 28.2 us -> 6.47 us
  local copies, waits for them, and re-layouts: 41.5 us -> 27.7 us
    all_to_all x17 -> x0, blocking collectives: 204 us -> none  [the longest x10 154 us: copy_for_each(): return lax.all_to_all(copies, axis, split_axis=0, concat_axis=0, tiled=True)]
    pallas_call x0 -> x7, Pallas kernels: none -> 154 us  [the longest x3 103 us: beam_step(): pl.pallas_call(functools.partial(beam_kernel, do_out, do_query, do_pages,...]
    reduce_scatter x1 -> x0, waiting for transfers between devices: 63.7 us -> none  [shards(): lax.psum_scatter(partial_out, 'heads', scatter_dimension=1, tiled=True)]
    all_to_all x6 -> x0, starting transfers between devices: 40.5 us -> none  [the longest x4 21.1 us: copy_for_each(): return lax.all_to_all(copies, axis, split_axis=0, concat_axis=0, tiled=True)]
    dot_general x14 -> x2, matrix products: 51.1 us -> 10.6 us  [the longest x1 6.67 us: shards(): jnp.dot(attended, lax.all_gather(out_weight, 'tokens', axis=1, tiled=True...]
    unnamed x3 -> x4, waiting for transfers between devices: 0.71 us -> 38.7 us
    all_to_all x6 -> x0, waiting for transfers between devices: 29.3 us -> none  [the longest x4 16.4 us: copy_for_each(): return lax.all_to_all(copies, axis, split_axis=0, concat_axis=0, tiled=True)]
    reduce_sum x18 -> x1, other arithmetic: 22.1 us -> 2.34 us  [shards(): factor = lax.rsqrt(jnp.mean(hidden_f * hidden_f, axis=1) + EPSILON)]
  transfers between devices with their start and end apart: 12 -> 7, of which waited for: 10 -> 2; matrix products, arithmetic and copies ran while one was open for 6% -> 8% of each run, Pallas kernels for 0% -> 14%
where the time goes in v1:
time: 311 us; the launch traced here: 310 us
  Pallas kernels  154 us (50%)
  waiting for transfers between devices  71.5 us (23%)
  local copies, waits for them, and re-layouts  27.7 us (9%)
  between operations  17.6 us (6%)
  matrix products  17.5 us (6%)
  starting transfers between devices  15.5 us (5%)
  other arithmetic  6.47 us (2%)
    pallas_call x3, Pallas kernels, beam_step(): pl.pallas_call(functools.partial(beam_kernel, do_out, do_query, do_pages,...  103 us
    pallas_call x3, Pallas kernels, attend(): pl.pallas_call(functools.partial(attend_kernel, blocks, block, fresh is n...  45.8 us
    unnamed x4, waiting for transfers between devices  38.7 us
    all_gather x1, waiting for transfers between devices, shards(): lax.all_gather(out_weight, 'tokens', axis=1, tiled=True)  32.8 us
    unnamed x59, local copies, waits for them, and re-layouts  18.6 us
    ppermute x4, starting transfers between devices, shards(): blocks.insert(0, lax.ppermute(keyvals, 'tokens', pairs))  15.2 us
    dot_general x1, matrix products, shards(): jnp.dot(attended, lax.all_gather(out_weight, 'tokens', axis=1, tiled=True...  6.67 us
  transfers between devices with their start and end apart: 7, of which 2 were waited for; matrix products, arithmetic and copies ran while one was open for 8% of the time, Pallas kernels for 14%

profile of v1, /device:TPU:1, one launch (start us, length us, event | category | flops | bytes accessed | tf_op | source)
XLA Modules:
  0.0 310.4 jit_solution(13230206787906454057)
XLA Ops:
  7.2 1.6 copy.106.cache_ref
  9.0 6.3 %collective-permute-start = (bf16[256,2,128]{2,0,1:T(8,128)(2,1)S(1)}, bf16[256,2,128]{2,0,1:T(8,128)(2,1)}, u32[]{:S(2)}, u32[]{:S(2)}) collective-permute-start(bf16[256,2,128]{2,0,1:T(8,128)(2,1)S(1)} %copy.62), channel_id=1, source_target_pairs={{0,4},{1,5},{2,6},{3,7},{4,8},{5,9},{6,10},{7,11},{8,12},{9,13},{1... | collective-permute-start | bytes 393224 | tf_op jit(solution)/shard_map/ppermute | solution.py:426
  15.3 3.8 %collective-permute-start.1 = (bf16[256,2,128]{2,0,1:T(8,128)(2,1)S(1)}, bf16[256,2,128]{2,0,1:T(8,128)(2,1)}, u32[]{:S(2)}, u32[]{:S(2)}) collective-permute-start(bf16[256,2,128]{2,0,1:T(8,128)(2,1)S(1)} %copy.62), channel_id=1, source_target_pairs={{0,3},{1,4},{2,5},{3,6},{4,7},{5,8},{6,9},{7,10},{8,11},{9,12},{10... | collective-permute-start | bytes 393224 | tf_op jit(solution)/shard_map/ppermute | solution.py:426
  19.0 3.2 %collective-permute-start.2 = (bf16[256,2,128]{2,0,1:T(8,128)(2,1)S(1)}, bf16[256,2,128]{2,0,1:T(8,128)(2,1)}, u32[]{:S(2)}, u32[]{:S(2)}) collective-permute-start(bf16[256,2,128]{2,0,1:T(8,128)(2,1)S(1)} %copy.62), channel_id=1, source_target_pairs={{0,2},{1,3},{2,4},{3,5},{4,6},{5,7},{6,8},{7,9},{8,10},{9,11},{10,... | collective-permute-start | bytes 393224 | tf_op jit(solution)/shard_map/ppermute | solution.py:426
  22.2 1.9 collective-permute-start.3
  24.2 1.0 and_and_fusion
  25.2 0.2 copy.67
  25.4 0.9 constant_dynamic-update-slice_fusion.4
  26.3 0.9 constant_dynamic-update-slice_fusion.3
  27.2 0.9 constant_dynamic-update-slice_fusion.2
  28.3 0.8 copy-done.18
  29.1 3.3 %fusion.49 = f32[5,256]{1,0:T(8,128)S(1)} fusion(pred[256,1280]{0,1:T(8,128)(4,1)S(1)} %and_and_fusion, bf16[256,5,128]{0,2,1:T(8,128)(2,1)S(1)} %bitcast.84, bf16[1280,2,128]{2,0,1:T(8,128)(2,1)} %copy-done.18), kind=kOutput, calls=%fused_computation.99 | convolution fusion | flops 425985280 | bytes 988160 | tf_op jit(solution)/shard_map/sub | solution.py:443
  32.4 4.0 %fusion.16 = bf16[128,5,256]{2,0,1:T(8,128)(2,1)S(1)} fusion(f32[5,256]{1,0:T(8,128)S(1)} %fusion.49, bf16[1280,2,128]{2,0,1:T(8,128)(2,1)} %copy-done.18, pred[256,1280]{0,1:T(8,128)(4,1)S(1)} %and_and_fusion, bf16[256,5,128]{0,2,1:T(8,128)(2,1)S(1)} %bitcast.85), kind=kOutput, calls=%fused_computation.24 | convolution fusion | flops 847219200 | bytes 1643520 | tf_op jit(solution)/shard_map/gts,sd->tgd/dot_general | solution.py:445
  36.4 32.8 %all-gather.3.cloned.1.call-done = bf16[640,5120]{0,1:T(8,128)(2,1)} async-done(((bf16[640,160]{0,1:T(8,128)(2,1)}), bf16[640,5120]{0,1:T(8,128)(2,1)}) %all-gather.3.cloned.1.call-update) | async-done | bytes 6553616 | tf_op jit(solution)/shard_map/all_gather | solution.py:452
  69.2 6.7 %convolution_convert_fusion = bf16[256,5120]{1,0:T(8,128)(2,1)} fusion(bf16[256,640]{0,1:T(8,128)(2,1)S(1)} %bitcast.89, bf16[640,5120]{0,1:T(8,128)(2,1)} %all-gather.3.cloned.1.call-done), kind=kOutput, calls=%fused_computation.8 | convolution fusion | flops 1679032320 | bytes 9502720 | tf_op jit(solution)/shard_map/dot_general | solution.py:450
  75.9 4.4 %copy.81 = bf16[256,5120]{0,1:T(8,128)(2,1)} copy(bf16[256,5120]{1,0:T(8,128)(2,1)} %convolution_convert_fusion) | data formatting | bytes 5242880
  80.3 0.2 all-gather.5.cloned.1.call-start
  80.6 38.6 %reduce-scatter.4.cloned.1.call-done = bf16[640,256]{1,0:T(8,128)(2,1)} async-done(((bf16[5120,256]{1,0:T(8,128)(2,1)}), bf16[640,256]{1,0:T(8,128)(2,1)}) %reduce-scatter.4.cloned.1.call-update) | async-done | bytes 327696
  119.2 1.2 copy.82
  120.5 0.7 copy-done.12
  121.2 0.8 pad_maximum_fusion
  122.0 0.5 slice.47
  126.4 3.0 fusion.45
  129.6 1.1 copy.98
  130.8 0.9 copy.85
  131.7 0.9 copy.86
  132.7 0.7 gather_fusion
  133.4 1.2 gather_fusion.1
  134.5 0.2 concatenate.18.refs_2_
  134.7 0.6 fusion.48
  135.4 1.8 slice_bitcast_fusion.12
  137.2 24.6 %beam_step_1.1.refs_0_ = bf16[256,640]{1,0:T(8,128)(2,1)S(1)} custom-call(bf16[8,32,160]{2,1,0:T(8,128)(2,1)S(1)} %broadcast_select_fusion.refs_0_.refs_3_, bf16[1,160]{1,0:T(2,128)(2,1)S(1)} %get-tuple-element.42.refs_1_, bf16[160,640]{1,0:T(8,128)(2,1)S(1)} %get-tuple-element.38.refs_2_), custom_call_target="tpu_custom_call" | custom-call | tf_op jit(solution)/shard_map/beam_step_1/pallas_call | solution.py:213
  161.8 0.6 compare_select_fusion.9.row_ref
  162.5 1.2 copy-done.4
  163.7 20.1 %attend_4_0.1 = (f32[256,1280]{1,0:T(8,128)S(1)}, f32[256,640]{1,0:T(8,128)S(1)}) custom-call(bf16[256,640]{1,0:T(8,128)(2,1)S(1)} %beam_step_1.1.refs_0_, bf16[4096,128]{1,0:T(8,128)(2,1)S(1)} %bitcast.73, bf16[4096,256]{1,0:T(8,128)(2,1)S(1)} %concatenate.18.refs_2_, f32[1,4096]{1,0:T(1,128)S(1)} %and_select_fusion.refs_3_), custom_call_target="tpu_custom_call" | custom-call | flops 2684354560 | bytes 3145728 | tf_op jit(solution)/shard_map/attend_4_0/pallas_call | solution.py:325
  183.9 0.7 copy-done.1
  184.6 0.8 copy-done.7
  185.4 2.3 fusion.2
  187.8 0.9 slice_convert_fusion
  188.7 3.6 %fusion.17 = bf16[256,256]{1,0:T(8,128)(2,1)S(1)} fusion(bf16[640,8,2,128]{3,2,1,0:T(2,128)(2,1)} %bitcast.88, f32[5120]{0:T(1024)S(1)} %bitcast.87, f32[256]{0:T(256)S(1)} %add_rsqrt_fusion, bf16[272,5120]{1,0:T(8,128)(2,1)} %all-gather.5.cloned.1.call-done), kind=kOutput, calls=%fused_computation.25 | convolution fusion | flops 676397056 | bytes 5395456 | tf_op jit(solution)/shard_map/dot_general | solution.py:465
  192.4 0.4 fusion.28.refs_6_
  192.9 3.0 attend_0_1.1
  196.0 46.8 %beam_step_2.1 = (bf16[8,32,160]{2,1,0:T(8,128)(2,1)S(1)}, bf16[256,640]{1,0:T(8,128)(2,1)S(1)}, bf16[32,16,256]{2,1,0:T(8,128)(2,1)S(1)}) custom-call(bf16[32,8,640]{2,1,0:T(8,128)(2,1)S(1)} %bitcast.77, f32[32,8,128]{2,1,0:T(8,128)S(1)} %bitcast.78, bf16[640,160]{1,0:T(8,128)(2,1)S(1)} %bitcast.72, ...), custom_call_target="tpu_custom_call" | custom-call | tf_op jit(solution)/shard_map/beam_step_2/pallas_call | solution.py:213
  242.8 22.6 %attend_4_1.1 = (bf16[256,640]{1,0:T(8,128)(2,1)S(1)}, f32[256,128]{1,0:T(8,128)S(1)}) custom-call(bf16[256,640]{1,0:T(8,128)(2,1)S(1)} %get-tuple-element.17.refs_0_, bf16[4096,128]{1,0:T(8,128)(2,1)S(1)} %bitcast.74, bf16[4096,256]{1,0:T(8,128)(2,1)S(1)} %concatenate.18.refs_2_, f32[1,4096]{1,0:T(1,128)S(1)} %and_select_fusion.refs_3_, ...), custom_call_target="tpu_custom_call" | custom-call | flops 2852126720 | bytes 3342336 | tf_op jit(solution)/shard_map/attend_4_1/pallas_call | solution.py:325
  265.4 31.1 %beam_step_3.1 = bf16[8,32,160]{2,1,0:T(8,128)(2,1)S(1)} custom-call(bf16[32,8,640]{2,1,0:T(8,128)(2,1)S(1)} %bitcast.76, f32[32,8,128]{2,1,0:T(8,128)S(1)} %bitcast.79, bf16[640,160]{1,0:T(8,128)(2,1)S(1)} %bitcast.71, bf16[8,32,160]{2,1,0:T(8,128)(2,1)S(1)} %get-tuple-element.20.refs_3_), custom_call_target="tpu_custom_call" | custom-call | tf_op jit(solution)/shard_map/beam_step_3/pallas_call | solution.py:213
  296.5 0.7 copy.76
  297.3 0.8 reshape.176.inbox_ref
  298.0 5.8 %place_pages.1 = bf16[4096,2,128]{2,1,0:T(2,128)(2,1)} custom-call(s32[32]{0:T(128)} %compare_select_fusion.9.row_ref, bf16[4096,2,128]{2,1,0:T(2,128)(2,1)} %copy-done.11, bf16[32,16,2,128]{3,2,1,0:T(2,128)(2,1)} %reshape.176.inbox_ref), custom_call_target="tpu_custom_call", output_to_operand_aliasing={{}: (1, {})} | custom-call | tf_op jit(solution)/shard_map/place_pages/pallas_call | solution.py:369
  (76 shorter events, 1.4 us)
Async XLA Ops:
  7.2 18.0 %copy-start.15 = (bf16[256,640]{1,0:T(8,128)(2,1)S(1)}, bf16[256,640]{1,0:T(8,128)(2,1)}, u32[]{:S(2)}) copy-start(bf16[256,640]{1,0:T(8,128)(2,1)} %param.15) | copy-start | bytes 983044
  7.2 1.8 copy-start.13
  7.2 62.0 %all-gather.3.cloned.1.call-start = ((), (), s32[]{:S(2)}) async-start(), calls=%async_computation.1 | async-start | bytes 6758400 | tf_op jit(solution)/shard_map/all_gather | solution.py:452
  8.9 117.6 %copy-start.11 = (bf16[4096,2,128]{2,1,0:T(2,128)(2,1)}, bf16[4096,2,128]{2,1,0:T(2,128)(2,1)S(1)}, u32[]{:S(2)}) copy-start(bf16[4096,2,128]{2,1,0:T(2,128)(2,1)S(1)} %copy.106.cache_ref) | copy-start | bytes 6291460
  8.9 110.3 %reduce-scatter.4.cloned.1.call-start = ((), (), s32[]{:S(2)}) async-start(), calls=%async_computation.3 | async-start | bytes 2949120
  9.0 16.4 %collective-permute-start = (bf16[256,2,128]{2,0,1:T(8,128)(2,1)S(1)}, bf16[256,2,128]{2,0,1:T(8,128)(2,1)}, u32[]{:S(2)}, u32[]{:S(2)}) collective-permute-start(bf16[256,2,128]{2,0,1:T(8,128)(2,1)S(1)} %copy.62), channel_id=1, source_target_pairs={{0,4},{1,5},{2,6},{3,7},{4,8},{5,9},{6,10},{7,11},{8,12},{9,13},{1... | collective-permute-start | bytes 393224 | tf_op jit(solution)/shard_map/ppermute | solution.py:426
  15.3 11.0 %collective-permute-start.1 = (bf16[256,2,128]{2,0,1:T(8,128)(2,1)S(1)}, bf16[256,2,128]{2,0,1:T(8,128)(2,1)}, u32[]{:S(2)}, u32[]{:S(2)}) collective-permute-start(bf16[256,2,128]{2,0,1:T(8,128)(2,1)S(1)} %copy.62), channel_id=1, source_target_pairs={{0,3},{1,4},{2,5},{3,6},{4,7},{5,8},{6,9},{7,10},{8,11},{9,12},{10... | collective-permute-start | bytes 393224 | tf_op jit(solution)/shard_map/ppermute | solution.py:426
  19.0 8.2 %collective-permute-start.2 = (bf16[256,2,128]{2,0,1:T(8,128)(2,1)S(1)}, bf16[256,2,128]{2,0,1:T(8,128)(2,1)}, u32[]{:S(2)}, u32[]{:S(2)}) collective-permute-start(bf16[256,2,128]{2,0,1:T(8,128)(2,1)S(1)} %copy.62), channel_id=1, source_target_pairs={{0,2},{1,3},{2,4},{3,5},{4,6},{5,7},{6,8},{7,9},{8,10},{9,11},{10,... | collective-permute-start | bytes 393224 | tf_op jit(solution)/shard_map/ppermute | solution.py:426
  22.2 5.9 %collective-permute-start.3 = (bf16[256,2,128]{2,0,1:T(8,128)(2,1)S(1)}, bf16[256,2,128]{2,0,1:T(8,128)(2,1)S(1)}, u32[]{:S(2)}, u32[]{:S(2)}) collective-permute-start(bf16[256,2,128]{2,0,1:T(8,128)(2,1)S(1)} %copy.62), channel_id=1, source_target_pairs={{0,1},{1,2},{2,3},{3,4},{4,5},{5,6},{6,7},{7,8},{8,9},{9,10},{10,1... | collective-permute-start | bytes 393224 | tf_op jit(solution)/shard_map/ppermute | solution.py:426
  28.3 0.8 copy-start.18
  75.8 44.5 %copy-start.16 = (bf16[256,640]{1,0:T(8,128)(2,1)S(1)}, bf16[256,640]{1,0:T(8,128)(2,1)}, u32[]{:S(2)}) copy-start(bf16[256,640]{1,0:T(8,128)(2,1)} %param.14) | copy-start | bytes 983044
  80.3 40.2 %copy-start.20 = (bf16[640]{0:T(1024)(128)(2,1)S(1)}, bf16[640]{0:T(1024)(128)(2,1)}, u32[]{:S(2)}) copy-start(bf16[640]{0:T(1024)(128)(2,1)} %param.18) | copy-start | bytes 3844
  80.3 41.7 %copy-start.10 = (s32[512]{0:T(512)S(1)}, s32[512]{0:T(512)}, u32[]{:S(2)}) copy-start(s32[512]{0:T(512)} %param.21) | copy-start | bytes 6148
  80.3 44.9 %copy-start.17 = (bf16[256,160]{0,1:T(8,128)(2,1)S(1)}, bf16[256,160]{0,1:T(8,128)(2,1)}, u32[]{:S(2)}) copy-start(bf16[256,160]{0,1:T(8,128)(2,1)} %param.23) | copy-start | bytes 245764
  80.3 45.0 %copy-start.21 = (s32[256]{0:T(256)S(1)}, s32[256]{0:T(256)}, u32[]{:S(2)}) copy-start(s32[256]{0:T(256)} %param.24) | copy-start | bytes 3076
  80.3 105.1 %all-gather.5.cloned.1.call-start = ((), (), s32[]{:S(2)}) async-start(), calls=%async_computation.2 | async-start | bytes 3133440 | tf_op jit(solution)/shard_map/all_gather | solution.py:460
  120.5 0.7 copy-start.12
  129.4 1.3 copy-start.14
  130.7 4.0 %copy-start.19 = (bf16[2,160]{1,0:T(2,128)(2,1)S(1)}, bf16[2,160]{1,0:T(2,128)(2,1)}, u32[]{:S(2)}) copy-start(bf16[2,160]{1,0:T(2,128)(2,1)} %param.25) | copy-start | bytes 1924
  162.5 1.2 copy-start.4
  183.8 0.7 copy-start.1
  184.6 0.8 copy-start.7
  188.7 4.2 %copy-start.2 = (bf16[256,640]{1,0:T(8,128)(2,1)S(1)}, bf16[256,640]{1,0:T(8,128)(2,1)}, u32[]{:S(2)}) copy-start(bf16[256,640]{1,0:T(8,128)(2,1)} %copy-done.1) | copy-start | bytes 983044
  188.7 4.2 %copy-start.8 = (f32[256,640]{1,0:T(8,128)S(1)}, f32[256,640]{1,0:T(8,128)}, u32[]{:S(2)}) copy-start(f32[256,640]{1,0:T(8,128)} %copy-done.7) | copy-start | bytes 1966084
  192.3 3.6 %copy-start.3 = (bf16[1,640,160]{2,1,0:T(8,128)(2,1)S(1)}, bf16[1,640,160]{2,1,0:T(8,128)(2,1)}, u32[]{:S(2)}) copy-start(bf16[1,640,160]{2,1,0:T(8,128)(2,1)} %copy.85) | copy-start | bytes 614404
  192.4 3.6 %copy-start.6 = (bf16[160,640]{1,0:T(8,128)(2,1)S(1)}, bf16[160,640]{1,0:T(8,128)(2,1)}, u32[]{:S(2)}) copy-start(bf16[160,640]{1,0:T(8,128)(2,1)} %get-tuple-element.37.refs_5_) | copy-start | bytes 614404
  192.4 3.6 %copy-start.9 = (bf16[1,160]{1,0:T(2,128)(2,1)S(1)}, bf16[1,160]{1,0:T(2,128)(2,1)}, u32[]{:S(2)}) copy-start(bf16[1,160]{1,0:T(2,128)(2,1)} %get-tuple-element.41.refs_4_) | copy-start | bytes 964
  192.4 50.4 %copy-start.5 = (bf16[4096,1,128]{2,0,1:T(8,128)(2,1)S(1)}, bf16[4096,1,128]{2,0,1:T(8,128)(2,1)}, u32[]{:S(2)}) copy-start(bf16[4096,1,128]{2,0,1:T(8,128)(2,1)} %copy.98) | copy-start | bytes 3145732
  242.7 22.6 %copy-start = (bf16[1,640,160]{2,1,0:T(8,128)(2,1)S(1)}, bf16[1,640,160]{2,1,0:T(8,128)(2,1)}, u32[]{:S(2)}) copy-start(bf16[1,640,160]{2,1,0:T(8,128)(2,1)} %copy.86) | copy-start | bytes 614404
Sparse Core Ops, SparseCore 0:
  10.5 58.5 all-gather.2
  80.5 38.7 reduce-scatter.3
  122.1 43.4 all-gather.4

commit v2 on v1

--- a/solution.py
+++ b/solution.py
@@ -236,54 +236,46 @@
         kf_ref, vf_ref = [refs.pop(0) for _ in range(2)]
     if has_carry:
         acc_in_ref, top_in_ref = [refs.pop(0) for _ in range(2)]
-    if last:
-        o_ref, lse_ref, acc, top = refs
-    else:
-        acc, top = refs
-    g = pl.program_id(0)
     q = q_ref[...]
     rows = q.shape[0]
     if has_carry:
-        acc[...] = acc_in_ref[...]
-        top[...] = top_in_ref[...]
+        acc, top = acc_in_ref[...], top_in_ref[:, :1]
     else:
-        acc[...] = jnp.zeros(acc.shape, jnp.float32)
-        top[...] = jnp.full(top.shape, -1e30, jnp.float32)
-
-    def step(keys, values, bias):
+        acc = jnp.zeros((rows, 2 * DH), jnp.float32)
+        top = jnp.full((rows, 1), -1e30, jnp.float32)
+
+    def step(acc, top, keys, values, bias):
         s = lax.dot_general(
             q, keys, (((1,), (1,)), ((), ())), preferred_element_type=jnp.float32
         )
         if bias is not None:
             s = s + bias
-        before = top[...]
-        here = jnp.maximum(before, jnp.max(s, axis=1, keepdims=True))
-        p = jnp.exp2((s - here[:, :1]) * SCALE2).astype(jnp.bfloat16)
-        shrink = jnp.exp2((before - here) * SCALE2)
-        top[...] = here
-        pv = jnp.dot(p, values, preferred_element_type=jnp.float32)
-        acc[...] = acc[...] * jnp.concatenate([shrink, shrink], axis=1) + pv
-
-    if blocks:
-
-        def body(b, carry):
-            at = pl.ds(pl.multiple_of(b * block, block), block)
-            step(k_ref[at, :], v_ref[at, :], bias_ref[:, at])
-            return carry
-
-        lax.fori_loop(0, blocks, body, 0)
+        here = jnp.maximum(top, jnp.max(s, axis=1, keepdims=True))
+        p = jnp.exp2((s - here) * SCALE2).astype(jnp.bfloat16)
+        shrink = jnp.exp2((top - here) * SCALE2)
+        return acc * shrink + jnp.dot(p, values, preferred_element_type=jnp.float32), here
+
+    for b in range(blocks):
+        at = slice(b * block, (b + 1) * block)
+        acc, top = step(acc, top, k_ref[at, :], v_ref[at, :], bias_ref[:, at])
     if has_fresh:
-        step(kf_ref[...], vf_ref[...], None)
+        acc, top = step(acc, top, kf_ref[...], vf_ref[...], None)
     if last:
+        o_ref, lse_ref = refs
+        g = pl.program_id(0)
         amount = acc[:, DH:]
         o_ref[...] = (acc[:, :DH] / amount).astype(jnp.bfloat16)
         lane = lax.broadcasted_iota(jnp.int32, (rows, DH), 1)
-        value = top[...] * SCALE2 + jnp.log2(amount)
+        value = top * SCALE2 + jnp.log2(amount)
         kept = jnp.where(g == 0, jnp.zeros_like(value), lse_ref[...])
         lse_ref[...] = jnp.where(lane == g, value, kept)
-
-
-def attend(q, old=None, fresh=None, carry=None, block=1024):
+    else:
+        acc_ref, top_ref = refs
+        acc_ref[...] = acc
+        top_ref[...] = jnp.broadcast_to(top, (rows, DH))
+
+
+def attend(q, old=None, fresh=None, carry=None, block=512):
     beams, width = q.shape
     groups = width // DH
     args, specs = [q], [pl.BlockSpec((beams, DH), lambda g: (0, g))]
@@ -310,17 +302,12 @@
             pl.BlockSpec((beams, DH), lambda g: (0, g)),
             pl.BlockSpec((beams, DH), lambda g: (0, 0)),
         ]
-        scratch = [
-            pltpu.VMEM((beams, 2 * DH), jnp.float32),
-            pltpu.VMEM((beams, DH), jnp.float32),
-        ]
     else:
         out_shape = [
             jax.ShapeDtypeStruct((beams, 2 * width), jnp.float32),
             jax.ShapeDtypeStruct((beams, width), jnp.float32),
         ]
         out_specs = [acc_spec, top_spec]
-        scratch = []
     rows = sum(a[0].shape[0] for a in (old, fresh) if a is not None)
     return pl.pallas_call(
         functools.partial(
@@ -330,7 +317,6 @@
         out_shape=out_shape,
         in_specs=specs,
         out_specs=out_specs,
-        scratch_shapes=scratch,
         compiler_params=pltpu.CompilerParams(vmem_limit_bytes=40 << 20),
         cost_estimate=pl.CostEstimate(
             flops=4 * beams * width * rows,
@@ -341,6 +327,552 @@
     )(*args)
 
 
+def fresh_kernel(
+    n_head,
+    subs,
+    subs2,
+    att_ref,
+    wt_hbm,
+    hid_ref,
+    gain_ref,
+    kvr_ref,
+    hid_out_ref,
+    fresh_ref,
+    wt,
+    part,
+    s_buf,
+    r_buf,
+    part2,
+    s_buf2,
+    r_buf2,
+    squares,
+    w_sems,
+    s_sems,
+    r_sems,
+    s_sems2,
+    r_sems2,
+    sq_sems,
+):
+    me = lax.axis_index("heads")
+    tokens, width = hid_ref.shape
+    half = tokens // 2
+    middle = n_head // 2
+    rows_sub = half // subs
+    rows_sub2 = tokens // subs2
+    wrap = lambda value: lax.rem(value + 2 * n_head, n_head)
+    lanes = [(sub, way) for sub in range(subs) for way in (0, 1)]
+    sign = (1, -1)
+    at_rows = lambda sub, way: slice(way * half + sub * rows_sub, way * half + (sub + 1) * rows_sub)
+
+    def load(c):
+        rows = pl.ds(pl.multiple_of(c * width, width), width)
+        return pltpu.make_async_copy(wt_hbm.at[rows], wt.at[c], w_sems.at[c])
+
+    lax.fori_loop(0, n_head, lambda c, k: (load(c).start(), k)[1], 0)
+    greet("heads", n_head, me)
+    pl.semaphore_wait(pltpu.get_barrier_semaphore(), n_head - 1)
+
+    def product(c):
+        load(c).wait()
+        part[c] = lax.dot_general(
+            att_ref[...], wt[c], (((1,), (1,)), ((), ())), preferred_element_type=jnp.float32
+        )
+
+    def sum_copy(step, sub, way):
+        return pltpu.make_async_remote_copy(
+            src_ref=s_buf.at[step, way, sub],
+            dst_ref=r_buf.at[step, way, sub],
+            send_sem=s_sems.at[step, way, sub],
+            recv_sem=r_sems.at[step, way, sub],
+            device_id={"heads": wrap(me + sign[way])},
+            device_id_type=MESH,
+        )
+
+    product(wrap(me - 1))
+    product(wrap(me + 1))
+
+    def reduce_step(step, carry):
+        for sub, way in lanes:
+            c = wrap(me - sign[way] * (1 + step))
+            own = part[c, at_rows(sub, way), :]
+
+            @pl.when(step == 0)
+            def _():
+                s_buf[step, way, sub] = own.astype(jnp.bfloat16)
+
+            @pl.when(step > 0)
+            def _():
+                sum_copy(step - 1, sub, way).wait_recv()
+                s_buf[step, way, sub] = (
+                    own + r_buf[step - 1, way, sub].astype(jnp.float32)
+                ).astype(jnp.bfloat16)
+
+            sum_copy(step, sub, way).start()
+
+        @pl.when(step < middle - 1)
+        def _():
+            product(wrap(me - 2 - step))
+            product(lax.select(step == middle - 2, me, wrap(me + 2 + step)))
+
+        return carry
+
+    lax.fori_loop(0, n_head - 1, reduce_step, 0)
+
+    last = n_head - 2
+    for sub, way in lanes:
+        rows = at_rows(sub, way)
+        sum_copy(last, sub, way).wait_recv()
+        total = part[me, rows, :] + r_buf[last, way, sub].astype(jnp.float32)
+        hid_out_ref[rows, :] = (hid_ref[rows, :].astype(jnp.float32) + total).astype(jnp.bfloat16)
+
+    hidden = hid_out_ref[...].astype(jnp.float32)
+    scaled = (hidden * gain_ref[...].astype(jnp.float32)).astype(jnp.bfloat16)
+
+    def product2(c):
+        part2[c] = jnp.dot(scaled, kvr_ref[c], preferred_element_type=jnp.float32)
+
+    count = (middle, n_head - 1 - middle)
+
+    def chunk(step, way):
+        return wrap(me + middle - step) if way == 0 else wrap(me - count[1] + step)
+
+    def share_copy(step, sub, way):
+        return pltpu.make_async_remote_copy(
+            src_ref=s_buf2.at[step, way, sub],
+            dst_ref=r_buf2.at[step, way, sub],
+            send_sem=s_sems2.at[step, way, sub],
+            recv_sem=r_sems2.at[step, way, sub],
+            device_id={"heads": wrap(me + sign[way])},
+            device_id_type=MESH,
+        )
+
+    product2(chunk(0, 0))
+    product2(chunk(0, 1))
+    for step in range(middle):
+        for sub in range(subs2):
+            rows = slice(sub * rows_sub2, (sub + 1) * rows_sub2)
+            for way in (0, 1):
+                if step >= count[way]:
+                    continue
+                value = part2[chunk(step, way), rows, :]
+                if step:
+                    share_copy(step - 1, sub, way).wait_recv()
+                    value = value + r_buf2[step - 1, way, sub].astype(jnp.float32)
+                s_buf2[step, way, sub] = value.astype(jnp.bfloat16)
+                share_copy(step, sub, way).start()
+        if step == 0:
+            flat = (hidden * hidden).astype(jnp.bfloat16)
+            ones = jnp.ones((8, width), jnp.bfloat16)
+            squares[me] = lax.dot_general(
+                ones, flat, (((1,), (1,)), ((), ())), preferred_element_type=jnp.float32
+            )
+            gather_start(squares, sq_sems, "heads", n_head, me)
+        for way in (0, 1):
+            if step + 1 < count[way]:
+                product2(chunk(step + 1, way))
+        if step == middle - 1:
+            product2(me)
+    finish(squares, sq_sems, "heads", n_head, me)
+    mean = jnp.transpose(jnp.sum(squares[...], axis=0))[:, :1] / D
+    factor = lax.rsqrt(mean + EPSILON)
+    for sub in range(subs2):
+        rows = slice(sub * rows_sub2, (sub + 1) * rows_sub2)
+        total = part2[me, rows, :]
+        for way in (0, 1):
+            share_copy(count[way] - 1, sub, way).wait_recv()
+            total = total + r_buf2[count[way] - 1, way, sub].astype(jnp.float32)
+        fresh_ref[rows, :] = (total * factor[rows]).astype(jnp.bfloat16)
+
+    def drain(step, carry):
+        for sub, way in lanes:
+            sum_copy(step, sub, way).wait_send()
+        return carry
+
+    lax.fori_loop(0, n_head - 1, drain, 0)
+    for way in (0, 1):
+        for step in range(count[way]):
+            for sub in range(subs2):
+                share_copy(step, sub, way).wait_send()
+
+
+def fresh_rows(n_head, attended, weight_t, hidden, gain, kvr, subs=2, subs2=2):
+    tokens, width = hidden.shape
+    bf16, f32 = jnp.bfloat16, jnp.float32
+    out_cols = kvr.shape[2]
+    pieces = (2, subs, tokens // 2 // subs, width)
+    pieces2 = (2, subs2, tokens // subs2, out_cols)
+    return pl.pallas_call(
+        functools.partial(fresh_kernel, n_head, subs, subs2),
+        out_shape=[
+            jax.ShapeDtypeStruct(hidden.shape, bf16),
+            jax.ShapeDtypeStruct((tokens, out_cols), bf16),
+        ],
+        in_specs=[VMEM_SPEC, pl.BlockSpec(memory_space=pl.ANY)] + [VMEM_SPEC] * 3,
+        out_specs=[VMEM_SPEC] * 2,
+        scratch_shapes=[
+            pltpu.VMEM((n_head, width, width), bf16),
+            pltpu.VMEM((n_head, tokens, width), f32),
+            pltpu.VMEM((n_head - 1, *pieces), bf16),
+            pltpu.VMEM((n_head - 1, *pieces), bf16),
+            pltpu.VMEM((n_head, tokens, out_cols), f32),
+            pltpu.VMEM((n_head // 2, *pieces2), bf16),
+            pltpu.VMEM((n_head // 2, *pieces2), bf16),
+            pltpu.VMEM((n_head, 8, tokens), f32),
+            pltpu.SemaphoreType.DMA((n_head,)),
+            pltpu.SemaphoreType.DMA((n_head - 1, 2, subs)),
+            pltpu.SemaphoreType.DMA((n_head - 1, 2, subs)),
+            pltpu.SemaphoreType.DMA((n_head // 2, 2, subs2)),
+            pltpu.SemaphoreType.DMA((n_head // 2, 2, subs2)),
+            pltpu.SemaphoreType.DMA((2,)),
+        ],
+        compiler_params=pltpu.CompilerParams(
+            collective_id=4, has_side_effects=True, vmem_limit_bytes=48 << 20
+        ),
+        name="fresh_rows",
+    )(attended, weight_t, hidden, gain[None, :], kvr)
+
+
+def entry_kernel(
+    n_tok,
+    n_head,
+    side,
+    state_ref,
+    gain_ref,
+    wq_ref,
+    own_w,
+    own_kv,
+    kvw,
+    q_out_ref,
+    whole_w,
+    win,
+    kvr,
+    q_send,
+    q_recv,
+    q_held,
+    q_sems,
+    w_sems,
+    pair_sems,
+    win_sems,
+    kv_sems,
+    kv_pair_sems,
+    local_sems,
+):
+    me = lax.axis_index("tokens")
+    me_h = lax.axis_index("heads")
+    core = lax.rem(me, 2)
+    y = lax.rem(me // 2, side)
+    x = me // (2 * side)
+    wide = n_tok // (2 * side)
+    partner = me + 1 - 2 * core
+    at = lambda i, j: (
+        lax.rem(x + i + 2 * wide, wide) * side + lax.rem(y + j + 2 * side, side)
+    ) * 2 + core
+    greet("tokens", n_tok, me)
+    greet("heads", n_head, me_h)
+    pl.semaphore_wait(pltpu.get_barrier_semaphore(), n_tok + n_head - 2)
+
+    state = state_ref[...].astype(jnp.float32)
+    squares = jnp.sum(state * state, axis=1, keepdims=True)
+    scaled = (state * gain_ref[...].astype(jnp.float32)).astype(jnp.bfloat16)
+    part = jnp.dot(scaled, wq_ref[...], preferred_element_type=jnp.float32)
+    width = part.shape[1]
+    rows = part.shape[0] // n_tok
+    q_send[:, :, :width] = part.reshape(n_tok, rows, width).astype(jnp.bfloat16)
+    q_send[:, :, width:] = (
+        jnp.broadcast_to(squares, (part.shape[0], DH)).reshape(n_tok, rows, DH).astype(jnp.bfloat16)
+    )
+    scatter_start(q_send, q_recv, q_sems.at[0], "tokens", n_tok, me)
+    q_recv[me] = q_send[me]
+
+    def remote(src, dst, sems, target, axis="tokens"):
+        return pltpu.make_async_remote_copy(
+            src_ref=src,
+            dst_ref=dst,
+            send_sem=sems.at[0],
+            recv_sem=sems.at[1],
+            device_id={axis: target},
+            device_id_type=MESH,
+        )
+
+    back = lambda b: lax.rem(me - b + n_tok, n_tok)
+    ahead = lambda b: lax.rem(me + b, n_tok)
+    win_two = remote(own_kv, win.at[2], win_sems.at[0], ahead(2))
+    win_four = remote(own_kv, win.at[4], win_sems.at[1], ahead(4))
+    win_two.start()
+    win_four.start()
+
+    depth = own_w.shape[0]
+    piece = depth // 4
+    block = lambda half, i, j: at(i, j) if half == 0 else at(j, i)
+
+    def rows_of(half, part_at=None):
+        if part_at is None:
+            return pl.ds(half * 2 * piece, 2 * piece)
+        return pl.ds((half * 2 + part_at) * piece, piece)
+
+    slots = {}
+    for half in (0, 1):
+        for name in ("a+", "a-", "f+", "f-"):
+            slots[half, name] = len(slots)
+        for i in (0, -1, 1, 2):
+            for name in ("a+", "a-", "f+", "f-"):
+                slots[half, i, name] = len(slots)
+
+    def first(half, name):
+        way = 1 if name[1] == "+" else -1
+        target = block(half, way, 0)
+        if name[0] == "a":
+            where = rows_of(half)
+            return remote(
+                own_w.at[where], whole_w.at[me, where], w_sems.at[slots[half, name]], target
+            )
+        ref = whole_w.at[block(half, -way, 0), rows_of(half, 0 if way == 1 else 1)]
+        return remote(ref, ref, w_sems.at[slots[half, name]], target)
+
+    def first_in(half, name):
+        way = 1 if name[1] == "+" else -1
+        if name[0] == "a":
+            ref = whole_w.at[block(half, -way, 0), rows_of(half)]
+        else:
+            ref = whole_w.at[block(half, -2 * way, 0), rows_of(half, 0 if way == 1 else 1)]
+        return remote(ref, ref, w_sems.at[slots[half, name]], block(half, way, 0))
+
+    def second(half, i, name):
+        way = 1 if name[1] == "+" else -1
+        target = block(half, 0, way)
+        if name[0] == "a":
+            where = rows_of(half)
+            dst = whole_w.at[block(half, i, 0), where]
+            src = own_w.at[where] if i == 0 else dst
+        else:
+            src = dst = whole_w.at[block(half, i, -way), rows_of(half, 0 if way == 1 else 1)]
+        return remote(src, dst, w_sems.at[slots[half, i, name]], target)
+
+    def second_in(half, i, name):
+        way = 1 if name[1] == "+" else -1
+        if name[0] == "a":
+            ref = whole_w.at[block(half, i, -way), rows_of(half)]
+        else:
+            ref = whole_w.at[block(half, i, -2 * way), rows_of(half, 0 if way == 1 else 1)]
+        return remote(ref, ref, w_sems.at[slots[half, i, name]], block(half, 0, way))
+
+    def share(half, i, j):
+        where = rows_of(half)
+        dst = whole_w.at[block(half, i, j), where]
+        src = own_w.at[where] if (i, j) == (0, 0) else dst
+        remote(src, dst, pair_sems, partner).start()
+
+    halves = (0, 1)
+    for half in halves:
+        for name in ("a+", "a-"):
+            first(half, name).start()
+    for half in halves:
+        for name in ("a+", "a-"):
+            second(half, 0, name).start()
+    for half in halves:
+        share(half, 0, 0)
+
+    kv_rows = kvw.shape[1] // 2
+    kv_half = pl.ds(pl.multiple_of(core * kv_rows, kv_rows), kv_rows)
+
+    def kv_out(k):
+        target = lax.rem(me_h + k, n_head)
+        return remote(
+            kvw.at[target, kv_half], kvr.at[me_h, kv_half], kv_sems.at[k - 1], target, "heads"
+        )
+
+    def kv_in(k):
+        ref = kvr.at[lax.rem(me_h - k + n_head, n_head), kv_half]
+        return remote(ref, ref, kv_sems.at[k - 1], lax.rem(me_h + k, n_head), "heads")
+
+    order = sorted(range(1, n_head), key=lambda k: min(k, n_head - k))
+    for k in order:
+        kv_out(k).start()
+
+    own_copies = [
+        pltpu.make_async_copy(own_w, whole_w.at[me], local_sems.at[0]),
+        pltpu.make_async_copy(own_kv, win.at[0], local_sems.at[1]),
+        pltpu.make_async_copy(kvw.at[me_h], kvr.at[me_h], local_sems.at[2]),
+    ]
+    for copy in own_copies:
+        copy.start()
+
+    finish(q_recv, q_sems.at[0], "tokens", n_tok, me)
+    total = jnp.sum(q_recv[...].astype(jnp.float32), axis=0)
+    factor = lax.rsqrt(total[:, width : width + 1] / D + EPSILON)
+    q_held[me] = (total[:, :width] * factor).astype(jnp.bfloat16)
+    gather_start(q_held, q_sems.at[1], "tokens", n_tok, me)
+
+    own_copies[1].wait()
+    win_in = lambda b, k: remote(win.at[b], win.at[b], win_sems.at[k], partner)
+
+    def relay(src, dst, k):
+        return remote(win.at[src], win.at[dst], win_sems.at[k], partner)
+
+    for name in ("a+", "a-"):
+        way = 1 if name[1] == "+" else -1
+        for half in halves:
+            first_in(half, name).wait_recv()
+            first(half, "f" + name[1]).start()
+            for other in ("a+", "a-"):
+                second(half, -way, other).start()
+            share(half, -way, 0)
+    win_in(2, 0).wait_recv()
+    relay(2 * core, 1, 2).start()
+    for name in ("a+", "a-"):
+        way = 1 if name[1] == "+" else -1
+        for half in halves:
+            second_in(half, 0, name).wait_recv()
+            second(half, 0, "f" + name[1]).start()
+            share(half, 0, -way)
+    for half in halves:
+        first_in(half, "f+").wait_recv()
+        first_in(half, "f-").wait_recv()
+        for other in ("a+", "a-"):
+            second(half, 2, other).start()
+        share(half, 2, 0)
+    win_in(4, 1).wait_recv()
+    relay(2 + 2 * core, 3, 3).start()
+    for i in (-1, 1):
+        for name in ("a+", "a-"):
+            way = 1 if name[1] == "+" else -1
+            for half in halves:
+                second_in(half, i, name).wait_recv()
+                second(half, i, "f" + name[1]).start()
+                share(half, i, -way)
+    finish(q_held, q_sems.at[1], "tokens", n_tok, me)
+    q_out_ref[...] = q_held[...].astype(jnp.float32).reshape(-1, width).astype(jnp.bfloat16)
+
+    def kv_share(k):
+        ref = kvr.at[lax.rem(me_h - k + n_head, n_head), kv_half]
+        return remote(ref, ref, kv_pair_sems.at[k - 1], partner)
+
+    def kv_share_in(k):
+        other = pl.ds(pl.multiple_of((1 - core) * kv_rows, kv_rows), kv_rows)
+        ref = kvr.at[lax.rem(me_h - k + n_head, n_head), other]
+        return remote(ref, ref, kv_pair_sems.at[k - 1], partner)
+
+    for k in order[: n_head // 2]:
+        kv_in(k).wait_recv()
+        kv_share(k).start()
+    for half in halves:
+        second_in(half, 0, "f+").wait_recv()
+        second_in(half, 0, "f-").wait_recv()
+        share(half, 0, 2)
+    for name in ("a+", "a-"):
+        way = 1 if name[1] == "+" else -1
+        for half in halves:
+            second_in(half, 2, name).wait_recv()
+            second(half, 2, "f" + name[1]).start()
+            share(half, 2, -way)
+    for i in (-1, 1, 2):
+        for half in halves:
+            second_in(half, i, "f+").wait_recv()
+            second_in(half, i, "f-").wait_recv()
+            share(half, i, 2)
+    for k in order[n_head // 2 :]:
+        kv_in(k).wait_recv()
+        kv_share(k).start()
+
+    win_in(1, 2).wait_recv()
+    win_in(3, 3).wait_recv()
+    relay(2 * core, 1, 2).wait_send()
+    relay(2 + 2 * core, 3, 3).wait_send()
+    win_two.wait_send()
+    win_four.wait_send()
+    for half in halves:
+        for name in ("a+", "a-", "f+", "f-"):
+            first(half, name).wait_send()
+            for i in (0, -1, 1, 2):
+                second(half, i, name).wait_send()
+    for k in order:
+        kv_out(k).wait_send()
+        kv_share(k).wait_send()
+        kv_share_in(k).wait_recv()
+    half_of_all = whole_w.at[pl.ds(0, n_tok // 2)]
+    remote(half_of_all, half_of_all, pair_sems, partner).wait()
+    own_copies[0].wait()
+    own_copies[2].wait()
+
+
+def entry(n_tok, n_head, state, gain, wq, own_w, own_kv, kvw, side=4):
+    bf16 = jnp.bfloat16
+    beams = state.shape[0]
+    width = wq.shape[1]
+    rows = beams // n_tok
+    any_spec = pl.BlockSpec(memory_space=pl.ANY)
+    reach = WINDOW // own_kv.shape[1] + 1
+    return pl.pallas_call(
+        functools.partial(entry_kernel, n_tok, n_head, side),
+        out_shape=[
+            jax.ShapeDtypeStruct((beams, width), bf16),
+            jax.ShapeDtypeStruct((n_tok, *own_w.shape), bf16),
+            jax.ShapeDtypeStruct((reach, *own_kv.shape), bf16),
+            jax.ShapeDtypeStruct(kvw.shape, bf16),
+        ],
+        in_specs=[VMEM_SPEC] * 3 + [any_spec] * 3,
+        out_specs=[VMEM_SPEC] + [any_spec] * 3,
+        scratch_shapes=[
+            pltpu.VMEM((n_tok, rows, width + DH), bf16),
+            pltpu.VMEM((n_tok, rows, width + DH), bf16),
+            pltpu.VMEM((n_tok, rows, width), bf16),
+            pltpu.SemaphoreType.DMA((2, 2)),
+            pltpu.SemaphoreType.DMA((40, 2)),
+            pltpu.SemaphoreType.DMA((2,)),
+            pltpu.SemaphoreType.DMA((4, 2)),
+            pltpu.SemaphoreType.DMA((n_head - 1, 2)),
+            pltpu.SemaphoreType.DMA((n_head - 1, 2)),
+            pltpu.SemaphoreType.DMA((3,)),
+        ],
+        compiler_params=pltpu.CompilerParams(
+            collective_id=1, has_side_effects=True, vmem_limit_bytes=16 << 20
+        ),
+        name="entry",
+    )(state, gain, wq, own_w, own_kv, kvw)
+
+
+def window_kernel(reach, q_ref, win_ref, bias_ref, o_ref):
+    q = q_ref[...]
+    rows = q.shape[0]
+    acc = jnp.zeros((rows, 2 * DH), jnp.float32)
+    top = jnp.full((rows, 1), -1e30, jnp.float32)
+    row = lax.broadcasted_iota(jnp.int32, (rows, rows), 0)
+    col = lax.broadcasted_iota(jnp.int32, (rows, rows), 1)
+    ones = jnp.ones((rows, DH), jnp.bfloat16)
+    for b in range(reach):
+        s = lax.dot_general(
+            q, win_ref[b, 0], (((1,), (1,)), ((), ())), preferred_element_type=jnp.float32
+        )
+        if b == 0:
+            s = jnp.where(col <= row, s, -1e30)
+        else:
+            s = s + bias_ref[:, b * rows : (b + 1) * rows]
+        if b == reach - 1:
+            s = jnp.where(col > row, s, -1e30)
+        here = jnp.maximum(top, jnp.max(s, axis=1, keepdims=True))
+        p = jnp.exp2((s - here) * SCALE2).astype(jnp.bfloat16)
+        shrink = jnp.exp2((top - here) * SCALE2)
+        values = jnp.concatenate([win_ref[b, 1], ones], axis=1)
+        acc = acc * shrink + jnp.dot(p, values, preferred_element_type=jnp.float32)
+        top = here
+    o_ref[...] = (acc[:, :DH] / acc[:, DH:]).astype(jnp.bfloat16)
+
+
+def window_attend(q, win, bias):
+    rows, width = q.shape
+    head = pl.BlockSpec((rows, DH), lambda g: (0, g))
+    whole = lambda a: pl.BlockSpec(a.shape, lambda g: (0,) * a.ndim)
+    return pl.pallas_call(
+        functools.partial(window_kernel, win.shape[0]),
+        grid=(width // DH,),
+        out_shape=jax.ShapeDtypeStruct(q.shape, jnp.bfloat16),
+        in_specs=[head, whole(win), whole(bias)],
+        out_specs=head,
+        compiler_params=pltpu.CompilerParams(vmem_limit_bytes=24 << 20),
+        name="window_attend",
+    )(q, win, bias)
+
+
 def place_kernel(page_rows, slots, row_ref, cache_ref, inbox_ref, out_ref, sem):
     def copy(slot):
         return pltpu.make_async_copy(
@@ -372,7 +904,7 @@
         in_specs=[
             pl.BlockSpec(memory_space=pltpu.SMEM),
             pl.BlockSpec(memory_space=pl.ANY),
-            pl.BlockSpec(memory_space=pl.ANY),
+            VMEM_SPEC,
         ],
         out_specs=pl.BlockSpec(memory_space=pl.ANY),
         scratch_shapes=[pltpu.SemaphoreType.DMA],
@@ -400,12 +932,20 @@
     n_tok = lax.axis_size("tokens")
     n_head = lax.axis_size("heads")
     tok_rows = hidden_in.shape[0]
-    head_local = queries.shape[1] // DH
     me = lax.axis_index("tokens")
     reach_back = -(-WINDOW // tok_rows)
 
     state = jnp.take(beam_state, parents, axis=0)
-    (q,) = beam_step(n_tok, n_head, 1, state, query=(beam_gain[0:1], query_weight[0]))
+    q, weight_t, win, kvr = entry(
+        n_tok,
+        n_head,
+        state,
+        beam_gain[0:1],
+        query_weight[0],
+        out_weight.T,
+        jnp.swapaxes(keyvals, 0, 1),
+        kv_weight.reshape(n_head, -1, 2 * DH),
+    )
 
     cache_rows = cache.shape[0]
     pages_here = cache_rows // PAGE
@@ -420,51 +960,12 @@
     old = (old_keys, old_values, bias)
     carry = attend(q, old=old)
 
-    blocks = [keyvals]
-    for back in range(1, reach_back + 1):
-        pairs = [(s, s + back) for s in range(n_tok - back)]
-        blocks.insert(0, lax.ppermute(keyvals, "tokens", pairs))
-    window_rows = jnp.concatenate(blocks, axis=0)
-    query_block = queries.reshape(tok_rows, head_local, DH)
-    scores = (
-        jnp.einsum(
-            "tgd,sd->gts", query_block, window_rows[:, 0], preferred_element_type=jnp.float32
-        )
-        * SCALE
+    back = jnp.arange(reach_back + 1, dtype=jnp.int32)
+    window_bias = jnp.repeat(jnp.where(back <= me, 0.0, -1e30).astype(jnp.float32), tok_rows)
+    attended = window_attend(queries, win, window_bias[None, :])
+    stretch_hidden, fresh = fresh_rows(
+        n_head, attended, weight_t.reshape(-1, weight_t.shape[2]), hidden_in, kv_gain, kvr
     )
-    query_pos = me * tok_rows + jnp.arange(tok_rows, dtype=jnp.int32)
-    key_pos = (me - reach_back) * tok_rows + jnp.arange(window_rows.shape[0], dtype=jnp.int32)
-    allowed = (
-        (key_pos[None, :] <= query_pos[:, None])
-        & (key_pos[None, :] > query_pos[:, None] - WINDOW)
-        & (key_pos[None, :] >= 0)
-    )
-    scores = jnp.where(allowed, scores, -1e30)
-    expo = jnp.exp(scores - jnp.max(scores, axis=-1, keepdims=True))
-    weights = (expo / jnp.sum(expo, axis=-1, keepdims=True)).astype(jnp.bfloat16)
-    attended = jnp.einsum(
-        "gts,sd->tgd", weights, window_rows[:, 1], preferred_element_type=jnp.float32
-    )
-    attended = attended.astype(jnp.bfloat16).reshape(tok_rows, head_local * DH)
-
-    partial_out = jnp.dot(
-        attended,
-        lax.all_gather(out_weight, "tokens", axis=1, tiled=True),
-        preferred_element_type=jnp.float32,
-    ).astype(jnp.bfloat16)
-    head_total = lax.psum_scatter(partial_out, "heads", scatter_dimension=1, tiled=True)
-    stretch_hidden = (
-        hidden_in.astype(jnp.float32) + head_total.astype(jnp.float32)
-    ).astype(jnp.bfloat16)
-    both = jnp.concatenate([stretch_hidden, jnp.tile(kv_gain[None, :], (16, 1))], axis=0)
-    both = lax.all_gather(both, "heads", axis=1, tiled=True)
-    hidden_f = both[:tok_rows].astype(jnp.float32)
-    gain_f = both[tok_rows].astype(jnp.float32)
-    factor = lax.rsqrt(jnp.mean(hidden_f * hidden_f, axis=1) + EPSILON)
-    full_rows = (hidden_f * factor[:, None] * gain_f).astype(jnp.bfloat16)
-    fresh = jnp.dot(
-        full_rows, kv_weight.reshape(kv_weight.shape[0], -1), preferred_element_type=jnp.float32
-    ).astype(jnp.bfloat16)
 
     own_pages = tok_rows // PAGE
     pages = fresh.reshape(own_pages, PAGE, -1)

time: 311 us -> 262 us (0.84)
  waiting for transfers between devices: 71.5 us -> 0 us
  Pallas kernels: 154 us -> 203 us
  local copies, waits for them, and re-layouts: 27.7 us -> 49.4 us
  matrix products: 17.5 us -> 0 us
  starting transfers between devices: 15.5 us -> 0 us
  between operations: 17.6 us -> 4.32 us
    pallas_call x0 -> x3, Pallas kernels: none -> 98.8 us  [the longest x1 48.1 us: fresh_rows(): pl.pallas_call(functools.partial(fresh_kernel, n_head, subs, subs2), out_...]
    unnamed x4 -> x0, waiting for transfers between devices: 38.7 us -> none
    all_gather x2 -> x0, waiting for transfers between devices: 32.8 us -> none  [the longest x1 32.8 us: shards(): lax.all_gather(out_weight, 'tokens', axis=1, tiled=True)]
    pallas_call x3, Pallas kernels: 45.8 us -> 19.4 us  [attend(): pl.pallas_call(functools.partial(attend_kernel, blocks, block, fresh is n...]
    pallas_call x3 -> x2, Pallas kernels: 103 us -> 82.4 us  [beam_step(): pl.pallas_call(functools.partial(beam_kernel, do_out, do_query, do_pages,...]
    unnamed x59 -> x91, local copies, waits for them, and re-layouts: 18.6 us -> 33.8 us
    ppermute x4 -> x0, starting transfers between devices: 15.2 us -> none  [shards(): blocks.insert(0, lax.ppermute(keyvals, 'tokens', pairs))]
    dot_general x3 -> x0, matrix products: 14.2 us -> none  [the longest x1 6.67 us: shards(): jnp.dot(attended, lax.all_gather(out_weight, 'tokens', axis=1, tiled=True...]
  transfers between devices with their start and end apart: 7 -> 0, of which waited for: 2 -> 0; matrix products, arithmetic and copies ran while one was open for 8% -> 0% of each run, Pallas kernels for 14% -> 0%
where the time goes in v2:
time: 262 us; the launch traced here: 261 us
  Pallas kernels  203 us (77%)
  local copies, waits for them, and re-layouts  49.4 us (19%)
  other arithmetic  4.44 us (2%)
  between operations  4.32 us (2%)
    pallas_call x2, Pallas kernels, beam_step(): pl.pallas_call(functools.partial(beam_kernel, do_out, do_query, do_pages,...  82.4 us
    pallas_call x1, Pallas kernels, fresh_rows(): pl.pallas_call(functools.partial(fresh_kernel, n_head, subs, subs2), out_...  48.1 us
    pallas_call x1, Pallas kernels, entry(): pl.pallas_call(functools.partial(entry_kernel, n_tok, n_head, side), out_...  46.9 us
    unnamed x91, local copies, waits for them, and re-layouts  33.8 us
    pallas_call x3, Pallas kernels, attend(): pl.pallas_call(functools.partial(attend_kernel, blocks, block, fresh is n...  19.4 us

profile of v2, /device:TPU:1, one launch (start us, length us, event | category | flops | bytes accessed | tf_op | source)
XLA Modules:
  0.0 260.7 jit_solution(10829388451220984956)
XLA Ops:
  0.7 4.5 %copy.52.cache_ref = bf16[4096,2,128]{2,1,0:T(2,128)(2,1)} copy(bf16[4096,2,128]{2,1,0:T(2,128)(2,1)} %param.20) | data formatting | bytes 4194304
  5.3 1.2 gather_fusion
  6.5 0.8 broadcast_select_fusion.state_ref
  7.8 0.7 slice_bitcast_fusion
  8.5 0.7 copy.47
  9.2 4.2 %reshape.139.kvw = bf16[8,640,256]{2,1,0:T(8,128)(2,1)S(1)} reshape(bf16[5120,2,128]{2,1,0:T(2,128)(2,1)} %param.19) | data formatting | bytes 5242880 | tf_op jit(solution)/shard_map/reshape | solution.py:947
  13.4 0.9 copy-done.8
  14.3 0.9 copy-done.9
  15.2 0.9 copy-done.20
  16.1 46.9 %entry.1 = (bf16[256,640]{1,0:T(8,128)(2,1)S(1)}, bf16[32,160,640]{2,1,0:T(8,128)(2,1)S(1)}, bf16[5,2,256,128]{3,2,1,0:T(8,128)(2,1)S(1)}, bf16[8,640,256]{2,1,0:T(8,128)(2,1)S(1)}) custom-call(bf16[256,160]{1,0:T(8,128)(2,1)S(1)} %copy-done.8, bf16[1,160]{1,0:T(2,128)(2,1)S(1)} %get-tuple-element.51.gain_ref, ...), custom_call_target="tpu_custom_call" | custom-call | tf_op jit(solution)/shard_map/entry/pallas_call | solution.py:805
  63.1 2.7 %copy-done = bf16[32,160,640]{2,1,0:T(8,128)(2,1)} copy-done((bf16[32,160,640]{2,1,0:T(8,128)(2,1)}, bf16[32,160,640]{2,1,0:T(8,128)(2,1)S(1)}, u32[]{:S(2)}) %copy-start) | copy-done | bytes 6553624
  65.8 1.6 copy-done.1
  67.4 0.7 copy-done.11
  68.2 1.0 copy-done.16
  69.1 3.8 %window_attend.1.att_ref = bf16[256,640]{1,0:T(8,128)(2,1)S(1)} custom-call(bf16[256,640]{1,0:T(8,128)(2,1)S(1)} %copy-done.16, bf16[5,2,256,128]{3,2,1,0:T(8,128)(2,1)S(1)} %get-tuple-element.18.win_ref, f32[1,1280]{1,0:T(1,128)S(1)} %bitcast.42), custom_call_target="tpu_custom_call" | custom-call | tf_op jit(solution)/shard_map/window_attend/pallas_call | solution.py:865
  73.0 1.7 copy-done.2
  74.7 1.0 copy-done.10
  75.7 48.1 %fresh_rows.1 = (bf16[256,640]{1,0:T(8,128)(2,1)S(1)}, bf16[256,256]{1,0:T(8,128)(2,1)S(1)}) custom-call(bf16[256,640]{1,0:T(8,128)(2,1)S(1)} %window_attend.1.att_ref, bf16[5120,640]{1,0:T(8,128)(2,1)} %bitcast.31, bf16[256,640]{1,0:T(8,128)(2,1)S(1)} %copy-done.10, bf16[1,640]{1,0:T(2,128)(2,1)S(1)} %broadcast_in_dim.69.gain_ref, ...), custom_call_target="tpu_custom_call" | custom-call | tf_op jit(solution)/shard_map/fresh_rows/pallas_call | solution.py:504
  123.8 0.7 copy-done.13
  127.7 0.7 gather_fusion.1
  129.1 3.0 %fusion.13 = (bf16[4096,1,128]{2,1,0:T(2,128)(2,1)S(1)}, bf16[4096,1,128]{2,1,0:T(2,128)(2,1)S(1)}) fusion(bf16[4096,2,128]{2,1,0:T(2,128)(2,1)S(1)} %copy-done.31), kind=kLoop, calls=%fused_computation.53 | loop fusion | bytes 4194304 | tf_op jit(solution)/shard_map/slice | solution.py:959
  133.7 1.0 copy-done.12
  134.6 8.2 %attend_8_0.1 = (f32[256,1280]{1,0:T(8,128)S(1)}, f32[256,640]{1,0:T(8,128)S(1)}) custom-call(bf16[256,640]{1,0:T(8,128)(2,1)S(1)} %copy-done.12, bf16[4096,128]{1,0:T(8,128)(2,1)S(1)} %get-tuple-element.53.refs_1_, bf16[4096,256]{1,0:T(8,128)(2,1)S(1)} %concatenate.10.refs_2_, f32[1,4096]{1,0:T(1,128)S(1)} %and_select_fusion.refs_3_), custom_call_target="tpu_custom_call" | custom-call | flops 2684354560 | bytes 3145728 | tf_op jit(solution)/shard_map/attend_8_0/pallas_call | solution.py:312
  142.8 3.2 %attend_0_1.1 = (bf16[256,640]{1,0:T(8,128)(2,1)S(1)}, f32[256,128]{1,0:T(8,128)S(1)}) custom-call(bf16[256,640]{1,0:T(8,128)(2,1)S(1)} %copy-done.12, bf16[256,128]{1,0:T(8,128)(2,1)S(1)} %get-tuple-element.49.refs_1_.refs_4_, bf16[256,256]{1,0:T(8,128)(2,1)S(1)} %concatenate.9.refs_2_.refs_5_, f32[256,1280]{1,0:T(8,128)S(1)} %get-tuple-element.24.refs_3_, ...), custom_call_target="tpu_custom_call" | custom-call | flops 167772160 | bytes 196608 | tf_op jit(solution)/shard_map/attend_0_1/pallas_call | solution.py:312
  146.1 0.9 fusion.14
  147.0 1.1 copy.41
  148.1 1.4 broadcast_in_dim.75
  149.4 1.7 broadcast_select_fusion.1.refs_3_
  151.1 1.2 fusion.3.refs_6_
  152.3 0.9 copy-done.3
  153.2 0.9 copy-done.7
  154.1 1.0 copy-done.18
  155.1 0.9 copy-done.22
  156.0 0.7 copy-done.27
  156.7 52.2 %beam_step_2.1 = (bf16[8,32,160]{2,1,0:T(8,128)(2,1)S(1)}, bf16[256,640]{1,0:T(8,128)(2,1)S(1)}, bf16[32,16,256]{2,1,0:T(8,128)(2,1)S(1)}) custom-call(bf16[32,8,640]{2,1,0:T(8,128)(2,1)S(1)} %bitcast.38, f32[32,8,128]{2,1,0:T(8,128)S(1)} %bitcast.40, bf16[640,160]{1,0:T(8,128)(2,1)S(1)} %bitcast.33, bf16[8,32,160]{2,1,0:T(8,128)(2,1)S(1)} %copy-done.7, ...), custom_call_target="tpu_custom_call" | custom-call | tf_op jit(solution)/shard_map/beam_step_2/pallas_call | solution.py:213
  208.9 0.7 copy-done.19
  210.3 0.7 copy-done.28
  211.0 1.7 reshape.144.inbox_ref
  212.7 2.0 place_pages.1
  214.7 1.0 copy-done.29
  215.6 8.0 %attend_8_1.1 = (bf16[256,640]{1,0:T(8,128)(2,1)S(1)}, f32[256,128]{1,0:T(8,128)S(1)}) custom-call(bf16[256,640]{1,0:T(8,128)(2,1)S(1)} %copy-done.29, bf16[4096,128]{1,0:T(8,128)(2,1)S(1)} %get-tuple-element.53.refs_1_, bf16[4096,256]{1,0:T(8,128)(2,1)S(1)} %concatenate.10.refs_2_, f32[1,4096]{1,0:T(1,128)S(1)} %and_select_fusion.refs_3_, ...), custom_call_target="tpu_custom_call" | custom-call | flops 2852126720 | bytes 3342336 | tf_op jit(solution)/shard_map/attend_8_1/pallas_call | solution.py:312
  223.7 0.7 copy-done.14
  225.0 1.1 copy.42
  226.2 1.0 copy-done.15
  227.1 0.9 copy-done.26
  228.0 30.2 %beam_step_3.1 = bf16[8,32,160]{2,1,0:T(8,128)(2,1)S(1)} custom-call(bf16[32,8,640]{2,1,0:T(8,128)(2,1)S(1)} %bitcast.37, f32[32,8,128]{2,1,0:T(8,128)S(1)} %bitcast.41, bf16[640,160]{1,0:T(8,128)(2,1)S(1)} %bitcast.32, bf16[8,32,160]{2,1,0:T(8,128)(2,1)S(1)} %copy-done.24), custom_call_target="tpu_custom_call" | custom-call | tf_op jit(solution)/shard_map/beam_step_3/pallas_call | solution.py:213
  258.2 0.7 copy.38
  259.0 1.7 copy.53
  (84 shorter events, 4.3 us)
Async XLA Ops:
  0.6 4.5 %copy-start.36 = (bf16[256,160]{0,1:T(8,128)(2,1)S(1)}, bf16[256,160]{0,1:T(8,128)(2,1)}, u32[]{:S(2)}) copy-start(bf16[256,160]{0,1:T(8,128)(2,1)} %param.23) | copy-start | bytes 245764
  0.6 4.6 %copy-start.39 = (s32[256]{0:T(256)S(1)}, s32[256]{0:T(256)}, u32[]{:S(2)}) copy-start(s32[256]{0:T(256)} %param.24) | copy-start | bytes 3076
  0.7 6.6 %copy-start.37 = (bf16[2,160]{1,0:T(2,128)(2,1)S(1)}, bf16[2,160]{1,0:T(2,128)(2,1)}, u32[]{:S(2)}) copy-start(bf16[2,160]{1,0:T(2,128)(2,1)} %param.25) | copy-start | bytes 1924
  0.7 7.2 %copy-start.33 = (bf16[2,160,640]{2,1,0:T(8,128)(2,1)S(1)}, bf16[2,160,640]{2,1,0:T(8,128)(2,1)}, u32[]{:S(2)}) copy-start(bf16[2,160,640]{2,1,0:T(8,128)(2,1)} %param.26) | copy-start | bytes 1228804
  5.2 3.4 %copy-start.35 = (bf16[256,2,128]{2,1,0:T(2,128)(2,1)S(1)}, bf16[256,2,128]{2,1,0:T(2,128)(2,1)}, u32[]{:S(2)}) copy-start(bf16[256,2,128]{2,1,0:T(2,128)(2,1)} %param.16) | copy-start | bytes 393220
  6.5 2.8 %copy-start.32 = (bf16[256,160]{1,0:T(8,128)(2,1)}, bf16[256,160]{1,0:T(8,128)(2,1)S(1)}, u32[]{:S(2)}) copy-start(bf16[256,160]{1,0:T(8,128)(2,1)S(1)} %gather_fusion) | copy-start | bytes 245764
  6.5 1.3 copy-start.40
  13.4 0.9 copy-start.8
  14.3 0.9 copy-start.9
  15.2 0.9 copy-start.20
  16.1 56.8 %copy-start.38 = (bf16[640]{0:T(1024)(128)(2,1)S(1)}, bf16[640]{0:T(1024)(128)(2,1)}, u32[]{:S(2)}) copy-start(bf16[640]{0:T(1024)(128)(2,1)} %param.18) | copy-start | bytes 3844
  63.1 2.7 %copy-start = (bf16[32,160,640]{2,1,0:T(8,128)(2,1)}, bf16[32,160,640]{2,1,0:T(8,128)(2,1)S(1)}, u32[]{:S(2)}) copy-start(bf16[32,160,640]{2,1,0:T(8,128)(2,1)S(1)} %get-tuple-element.19) | copy-start | bytes 19660804
  65.8 1.6 copy-start.1
  67.4 0.7 copy-start.11
  68.2 1.0 copy-start.16
  73.0 1.7 copy-start.2
  74.7 1.0 copy-start.10
  75.7 48.8 %copy-start.30 = (s32[512]{0:T(512)S(1)}, s32[512]{0:T(512)}, u32[]{:S(2)}) copy-start(s32[512]{0:T(512)} %param.21) | copy-start | bytes 6148
  75.7 53.4 %copy-start.31 = (bf16[4096,2,128]{2,1,0:T(2,128)(2,1)S(1)}, bf16[4096,2,128]{2,1,0:T(2,128)(2,1)}, u32[]{:S(2)}) copy-start(bf16[4096,2,128]{2,1,0:T(2,128)(2,1)} %copy.52.cache_ref) | copy-start | bytes 6291460
  123.8 0.7 copy-start.13
  124.5 7.5 %copy-start.4 = (bf16[256,256]{1,0:T(8,128)(2,1)}, bf16[256,256]{1,0:T(8,128)(2,1)S(1)}, u32[]{:S(2)}) copy-start(bf16[256,256]{1,0:T(8,128)(2,1)S(1)} %get-tuple-element.23) | copy-start | bytes 393220
  129.1 13.8 %copy-start.5 = (bf16[256,256]{1,0:T(8,128)(2,1)}, bf16[256,256]{1,0:T(8,128)(2,1)S(1)}, u32[]{:S(2)}) copy-start(bf16[256,256]{1,0:T(8,128)(2,1)S(1)} %concatenate.9.refs_2_.refs_5_) | copy-start | bytes 393220
  133.7 1.0 copy-start.12
  142.8 3.2 %copy-start.34 = (bf16[2,640,160]{1,2,0:T(8,128)(2,1)S(1)}, bf16[2,640,160]{1,2,0:T(8,128)(2,1)}, u32[]{:S(2)}) copy-start(bf16[2,640,160]{1,2,0:T(8,128)(2,1)} %param.27) | copy-start | bytes 1228804
  146.0 0.9 copy-start.17
  146.1 0.9 copy-start.21
  152.3 0.9 copy-start.3
  153.2 0.9 copy-start.7
  154.1 1.0 copy-start.18
  155.1 0.9 copy-start.22
  156.0 0.7 copy-start.27
  208.9 0.7 copy-start.19
  209.6 0.7 copy-start.23
  210.3 0.7 copy-start.28
  212.7 2.0 copy-start.6
  214.7 1.0 copy-start.29
  215.6 10.5 %copy-start.24 = (bf16[8,32,160]{2,1,0:T(8,128)(2,1)S(1)}, bf16[8,32,160]{2,1,0:T(8,128)(2,1)}, u32[]{:S(2)}) copy-start(bf16[8,32,160]{2,1,0:T(8,128)(2,1)} %copy-done.23) | copy-start | bytes 245764
  223.6 0.7 copy-start.14
  224.4 0.6 copy-start.25
  226.1 1.0 copy-start.15
  227.1 0.9 copy-start.26

commit v3 on v2

v3 whole, which is shorter than its diff:
```python
import functools
import math

import jax
import jax.numpy as jnp
from jax import lax
from jax.experimental import pallas as pl
from jax.experimental.pallas import tpu as pltpu
from jax.sharding import PartitionSpec as P

D = 5120
DH = 128
WINDOW = 1024
PAGE = 16
LAYERS = 2
EPSILON = 1e-06
SCALE = DH ** (-0.5)
SCALE2 = SCALE * math.log2(math.e)
MESH = pl.DeviceIdType.MESH
VMEM_SPEC = pl.BlockSpec(memory_space=pltpu.VMEM)


def scatter_start(send, recv, sems, axis, count, me):
    def one(step, carry):
        peer = lax.rem(me + step, count)
        pltpu.make_async_remote_copy(
            src_ref=send.at[peer],
            dst_ref=recv.at[me],
            send_sem=sems.at[0],
            recv_sem=sems.at[1],
            device_id={axis: peer},
            device_id_type=MESH,
        ).start()
        return carry

    lax.fori_loop(1, count, one, 0)


def gather_start(held, sems, axis, count, me):
    def one(step, carry):
        peer = lax.rem(me + step, count)
        pltpu.make_async_remote_copy(
            src_ref=held.at[me],
            dst_ref=held.at[me],
            send_sem=sems.at[0],
            recv_sem=sems.at[1],
            device_id={axis: peer},
            device_id_type=MESH,
        ).start()
        return carry

    lax.fori_loop(1, count, one, 0)


def finish(held, sems, axis, count, me):
    everything = held.at[pl.ds(0, count - 1)]
    pltpu.make_async_remote_copy(
        src_ref=everything,
        dst_ref=everything,
        send_sem=sems.at[0],
        recv_sem=sems.at[1],
        device_id={axis: lax.rem(me + 1, count)},
        device_id_type=MESH,
    ).wait()


def greet(axis, count, me):
    barrier = pltpu.get_barrier_semaphore()

    def one(step, carry):
        pl.semaphore_signal(
            barrier, inc=1, device_id={axis: lax.rem(me + step, count)}, device_id_type=MESH
        )
        return carry

    lax.fori_loop(1, count, one, 0)


def page_slot(home_ref, me, own_pages, pages_here, n_tok, slot):
    shift = lax.div(home_ref[0], pages_here)
    which = lax.rem(me - shift - own_pages * slot + 2 * n_tok * own_pages, n_tok)
    page = home_ref[own_pages * slot + jnp.minimum(which, own_pages - 1)]
    return jnp.where(which < own_pages, lax.rem(page, pages_here), -1)


def rest_kernel(
    n_tok,
    n_head,
    subs,
    subs2,
    block,
    split_at,
    home_ref,
    len_ref,
    att_ref,
    hid_ref,
    gain_ref,
    q_ref,
    state_ref,
    beam_gain_ref,
    wt_hbm,
    kvr_hbm,
    keys_hbm,
    values_hbm,
    wo_hbm,
    wq_hbm,
    hid_out_ref,
    inbox_ref,
    state_out_ref,
    wt,
    part,
    s_buf,
    r_buf,
    part2,
    s_buf2,
    r_buf2,
    squares,
    kvi,
    kvd,
    spread,
    keys,
    values,
    wo,
    wq,
    bias,
    acc_s,
    top_s,
    fk,
    fv,
    pages,
    outbox,
    inbox,
    lse_s,
    oa_send,
    ob_send,
    oa_recv,
    ob_recv,
    oa_held,
    ob_held,
    b_send,
    b_recv,
    s_held,
    q_send,
    q_recv,
    qa_held,
    qb_held,
    load_sems,
    w_sems,
    s_sems,
    r_sems,
    s_sems2,
    r_sems2,
    sq_sems,
    page_sems,
    tok_sems,
    head_sems,
):
    f32, bf16 = jnp.float32, jnp.bfloat16
    me = lax.axis_index("heads")
    me_t = lax.axis_index("tokens")
    tok = ("tokens", n_tok, me_t)
    head = ("heads", n_head, me)
    tokens, width = hid_ref.shape
    heads_here = width // DH
    half = tokens // 2
    middle = n_head // 2
    rows_sub = half // subs
    rows_sub2 = tokens // subs2
    wrap = lambda value: lax.rem(value + 2 * n_head, n_head)
    lanes = [(sub, way) for sub in range(subs) for way in (0, 1)]
    sign = (1, -1)
    at_rows = lambda sub, way: slice(way * half + sub * rows_sub, way * half + (sub + 1) * rows_sub)

    def load(c):
        rows = pl.ds(pl.multiple_of(c * width, width), width)
        return pltpu.make_async_copy(wt_hbm.at[rows], wt.at[c], w_sems.at[c])

    lax.fori_loop(0, n_head, lambda c, k: (load(c).start(), k)[1], 0)
    loads = [
        pltpu.make_async_copy(src, dst, load_sems.at[k])
        for k, (src, dst) in enumerate(
            [(kvr_hbm, kvi), (keys_hbm, keys), (values_hbm, values), (wo_hbm, wo), (wq_hbm, wq)]
        )
    ]
    for copy in loads:
        copy.start()
    greet(*head)
    greet(*tok)

    cache_rows = keys.shape[0]
    pages_here = cache_rows // PAGE
    own_pages = tokens // PAGE
    lane = lax.broadcasted_iota(jnp.int32, (1, cache_rows), 1)
    kept = (me_t * cache_rows + lane) < len_ref[0]
    page_of = lane // PAGE
    for slot in range(n_tok):
        landing = page_slot(home_ref, me_t, own_pages, pages_here, n_tok, slot)
        kept = kept & (page_of != landing)
    bias[...] = jnp.where(kept, 0.0, -1e30).astype(f32)

    pl.semaphore_wait(pltpu.get_barrier_semaphore(), n_head + n_tok - 2)

    def product(c):
        load(c).wait()
        part[c] = lax.dot_general(
            att_ref[...], wt[c], (((1,), (1,)), ((), ())), preferred_element_type=f32
        )

    def sum_copy(step, sub, way):
        return pltpu.make_async_remote_copy(
            src_ref=s_buf.at[step, way, sub],
            dst_ref=r_buf.at[step, way, sub],
            send_sem=s_sems.at[step, way, sub],
            recv_sem=r_sems.at[step, way, sub],
            device_id={"heads": wrap(me + sign[way])},
            device_id_type=MESH,
        )

    def soft(q, acc, top, keys_b, values_b, bias_b):
        s = lax.dot_general(q, keys_b, (((1,), (1,)), ((), ())), preferred_element_type=f32)
        if bias_b is not None:
            s = s + bias_b
        here = jnp.maximum(top, jnp.max(s, axis=1, keepdims=True))
        p = jnp.exp2((s - here) * SCALE2).astype(bf16)
        shrink = jnp.exp2((top - here) * SCALE2)
        both = jnp.concatenate([values_b, jnp.ones_like(values_b)], axis=1)
        return acc * shrink + jnp.dot(p, both, preferred_element_type=f32), here

    def soft_old(q):
        acc = jnp.zeros((q.shape[0], 2 * DH), f32)
        top = jnp.full((q.shape[0], 1), -1e30, f32)
        for b in range(cache_rows // block):
            at = slice(b * block, (b + 1) * block)
            acc, top = soft(q, acc, top, keys[at, :], values[at, :], bias[:, at])
        return acc, top

    def spread_kv(c):
        spread[...] = kvi[c].astype(f32)
        count = width
        kvd[c, :, :DH] = spread[pl.ds(0, count, stride=2), :].astype(bf16)
        kvd[c, :, DH:] = spread[pl.ds(1, count, stride=2), :].astype(bf16)

    product(wrap(me - 1))
    product(wrap(me + 1))

    def reduce_step(step, carry):
        for sub, way in lanes:
            c = wrap(me - sign[way] * (1 + step))
            own = part[c, at_rows(sub, way), :]

            @pl.when(step == 0)
            def _():
                s_buf[step, way, sub] = own.astype(bf16)

            @pl.when(step > 0)
            def _():
                sum_copy(step - 1, sub, way).wait_recv()
                s_buf[step, way, sub] = (own + r_buf[step - 1, way, sub].astype(f32)).astype(bf16)

            sum_copy(step, sub, way).start()

        @pl.when(step < middle - 1)
        def _():
            product(wrap(me - 2 - step))
            product(lax.select(step == middle - 2, me, wrap(me + 2 + step)))

        @pl.when(step == 1)
        def _():
            for copy in loads:
                copy.wait()

        @pl.when(step >= n_head - 1 - heads_here)
        def _():
            g = jnp.maximum(step - (n_head - 1 - heads_here), 0)
            q = q_ref[:, pl.ds(pl.multiple_of(g * DH, DH), DH)]
            acc, top = soft_old(q)
            acc_s[g] = acc
            top_s[g] = jnp.broadcast_to(top, (top.shape[0], DH))

        @pl.when(step >= middle - 1)
        def _():
            first = (step - (middle - 1)) * 2
            spread_kv(first)
            spread_kv(first + 1)

        return carry

    lax.fori_loop(0, n_head - 1, reduce_step, 0)

    last = n_head - 2
    for sub, way in lanes:
        rows = at_rows(sub, way)
        sum_copy(last, sub, way).wait_recv()
        total = part[me, rows, :] + r_buf[last, way, sub].astype(f32)
        hid_out_ref[rows, :] = (hid_ref[rows, :].astype(f32) + total).astype(bf16)

    hidden = hid_out_ref[...].astype(f32)
    scaled = (hidden * gain_ref[...].astype(f32)).astype(bf16)

    def product2(c):
        part2[c] = jnp.dot(scaled, kvd[c], preferred_element_type=f32)

    count = (middle, n_head - 1 - middle)

    def chunk(step, way):
        return wrap(me + middle - step) if way == 0 else wrap(me - count[1] + step)

    def share_copy(step, sub, way):
        return pltpu.make_async_remote_copy(
            src_ref=s_buf2.at[step, way, sub],
            dst_ref=r_buf2.at[step, way, sub],
            send_sem=s_sems2.at[step, way, sub],
            recv_sem=r_sems2.at[step, way, sub],
            device_id={"heads": wrap(me + sign[way])},
            device_id_type=MESH,
        )

    product2(chunk(0, 0))
    product2(chunk(0, 1))
    for step in range(middle):
        for sub in range(subs2):
            rows = slice(sub * rows_sub2, (sub + 1) * rows_sub2)
            for way in (0, 1):
                if step >= count[way]:
                    continue
                value = part2[chunk(step, way), rows, :]
                if step:
                    share_copy(step - 1, sub, way).wait_recv()
                    value = value + r_buf2[step - 1, way, sub].astype(f32)
                s_buf2[step, way, sub] = value.astype(bf16)
                share_copy(step, sub, way).start()
        if step == 0:
            flat = (hidden * hidden).astype(bf16)
            ones = jnp.ones((8, width), bf16)
            squares[me] = lax.dot_general(
                ones, flat, (((1,), (1,)), ((), ())), preferred_element_type=f32
            )
            gather_start(squares, sq_sems, *head)
        for way in (0, 1):
            if step + 1 < count[way]:
                product2(chunk(step + 1, way))
        if step == middle - 1:
            product2(me)
    finish(squares, sq_sems, *head)
    mean = jnp.transpose(jnp.sum(squares[...], axis=0))[:, :1] / D
    factor = lax.rsqrt(mean + EPSILON)
    for sub in range(subs2):
        rows = slice(sub * rows_sub2, (sub + 1) * rows_sub2)
        total = part2[me, rows, :]
        for way in (0, 1):
            share_copy(count[way] - 1, sub, way).wait_recv()
            total = total + r_buf2[count[way] - 1, way, sub].astype(f32)
        fresh = total * factor[rows]
        fk[rows, :] = fresh[:, :DH].astype(bf16)
        fv[rows, :] = fresh[:, DH:].astype(bf16)

    lane8 = lax.broadcasted_iota(jnp.int32, (tokens, DH), 1)
    sends = (oa_send, ob_send)
    spans = ((0, split_at), (split_at, heads_here))

    def put_head(layer, group, g, acc, top):
        amount = acc[:, DH:]
        out = (acc[:, :DH] / amount).reshape(n_tok, -1, DH).astype(bf16)
        at = pl.multiple_of((g - spans[group][0]) * DH, DH)
        sends[group][layer, :, :, pl.ds(at, DH)] = out
        value = top * SCALE2 + jnp.log2(amount)
        mine = (lane8 % 8 == g) & (lane8 < 24)
        lse_s[...] = jnp.where(mine, value, lse_s[...])

    def send_group(layer, group):
        value = lse_s[...]
        high = value.astype(bf16).astype(f32)
        mid = (value - high).astype(bf16).astype(f32)
        low = value - high - mid
        packed = jnp.where(lane8 < 8, high, jnp.where(lane8 < 16, mid, low))
        wide = (spans[group][1] - spans[group][0]) * DH
        sends[group][layer, :, :, wide:] = packed.reshape(n_tok, -1, DH).astype(bf16)
        recv = (oa_recv, ob_recv)[group].at[layer]
        scatter_start(sends[group].at[layer], recv, tok_sems.at[layer, group], *tok)

    def mix_group(layer, group):
        recv = (oa_recv, ob_recv)[group].at[layer]
        held = (oa_held, ob_held)[group].at[layer]
        low, high = spans[group]
        wide = (high - low) * DH
        recv[me_t] = sends[group][layer, me_t]
        finish(recv, tok_sems.at[layer, group], *tok)
        packed = recv[:, :, wide:].astype(f32)
        lse = (
            packed[:, :, low:high]
            + packed[:, :, 8 + low : 8 + high]
            + packed[:, :, 16 + low : 16 + high]
        )
        weight = jnp.exp2(lse - jnp.max(lse, axis=0, keepdims=True))
        share = weight / jnp.sum(weight, axis=0, keepdims=True)
        for k in range(high - low):
            cols = slice(k * DH, (k + 1) * DH)
            mixed = jnp.sum(recv[:, :, cols].astype(f32) * share[:, :, k : k + 1], axis=0)
            held[me_t, :, cols] = mixed.astype(bf16)
        gather_start(held, tok_sems.at[layer, 2 + group], *tok)

    def branch_of(layer, group):
        held = (oa_held, ob_held)[group].at[layer]
        finish(held, tok_sems.at[layer, 2 + group], *tok)
        low, high = spans[group]
        wide = (high - low) * DH
        whole = held[...].astype(f32).reshape(-1, wide).astype(bf16)
        return lax.dot_general(
            whole,
            wo[layer, :, low * DH : high * DH],
            (((1,), (1,)), ((), ())),
            preferred_element_type=f32,
        )

    def project(layer, before):
        mix_group(layer, 0)
        mix_group(layer, 1)
        branch = branch_of(layer, 0) + branch_of(layer, 1)
        send, recv, held = b_send.at[layer], b_recv.at[layer], s_held.at[layer]
        send[...] = branch.reshape(send.shape).astype(bf16)
        scatter_start(send, recv, head_sems.at[layer, 0], *head)
        recv[me] = send[me]
        finish(recv, head_sems.at[layer, 0], *head)
        total = jnp.sum(recv[...].astype(f32), axis=0)
        held[me] = (before[me].astype(f32) + total).astype(bf16)
        gather_start(held, head_sems.at[layer, 1], *head)
        finish(held, head_sems.at[layer, 1], *head)

    lse_s[...] = jnp.zeros(lse_s.shape, f32)
    for group in (0, 1):
        for g in range(*spans[group]):
            q = q_ref[:, g * DH : (g + 1) * DH]
            acc, top = soft(q, acc_s[g], top_s[g][:, :1], fk[...], fv[...], None)
            put_head(0, group, g, acc, top)
        send_group(0, group)

    spread[pl.ds(0, tokens, stride=2), :] = fk[...].astype(f32)
    spread[pl.ds(1, tokens, stride=2), :] = fv[...].astype(f32)
    pages[0:own_pages] = spread[0 : 2 * tokens, :].reshape(own_pages, -1, DH).astype(bf16)
    pages[own_pages:] = jnp.zeros((n_tok - own_pages, *pages.shape[1:]), bf16)
    shift = lax.div(home_ref[0], pages_here)

    def stage(peer, carry):
        which = lax.rem(peer - shift - own_pages * me_t + 2 * n_tok * own_pages, n_tok)
        outbox[peer] = pages[which]
        return carry

    lax.fori_loop(0, n_tok, stage, 0)
    scatter_start(outbox, inbox, page_sems, *tok)
    inbox[me_t] = outbox[me_t]

    project(0, state_ref)
    state = s_held[0].astype(f32).reshape(tokens, -1)
    sq = jnp.sum(state * state, axis=1, keepdims=True)
    scaled = (state * beam_gain_ref[...].astype(f32)).astype(bf16)
    share_q = jnp.dot(scaled, wq[...], preferred_element_type=f32)
    rows = tokens // n_tok
    q_send[:, :, :width] = share_q.reshape(n_tok, rows, width).astype(bf16)
    q_send[:, :, width:] = jnp.broadcast_to(sq, (tokens, DH)).reshape(n_tok, rows, DH).astype(bf16)
    scatter_start(q_send, q_recv, tok_sems.at[2, 0], *tok)
    q_recv[me_t] = q_send[me_t]
    finish(q_recv, tok_sems.at[2, 0], *tok)
    total = jnp.sum(q_recv[...].astype(f32), axis=0)
    scale = lax.rsqrt(total[:, width : width + 1] / D + EPSILON)
    ready = (total[:, :width] * scale).astype(bf16)
    cut = split_at * DH
    qa_held[me_t] = ready[:, :cut]
    gather_start(qa_held, tok_sems.at[2, 1], *tok)
    qb_held[me_t] = ready[:, cut:]
    gather_start(qb_held, tok_sems.at[2, 2], *tok)
    for group, held in ((0, qa_held), (1, qb_held)):
        finish(held, tok_sems.at[2, 1 + group], *tok)

        def one_head(g, carry, group=group, held=held):
            at = pl.multiple_of((g - spans[group][0]) * DH, DH)
            q = held[:, :, pl.ds(at, DH)].astype(f32).reshape(-1, DH).astype(bf16)
            acc, top = soft_old(q)
            acc, top = soft(q, acc, top, fk[...], fv[...], None)
            put_head(1, group, g, acc, top)
            return carry

        lax.fori_loop(*spans[group], one_head, 0)
        send_group(1, group)
    project(1, s_held.at[0])
    state_out_ref[...] = s_held[1]
    finish(inbox, page_sems, *tok)
    inbox_ref[...] = inbox[...]

    def drain(step, carry):
        for sub, way in lanes:
            sum_copy(step, sub, way).wait_send()
        return carry

    lax.fori_loop(0, n_head - 1, drain, 0)
    for way in (0, 1):
        for step in range(count[way]):
            for sub in range(subs2):
                share_copy(step, sub, way).wait_send()


def rest(
    n_tok,
    n_head,
    page_home,
    cache_len,
    attended,
    hidden,
    gain,
    q,
    state,
    beam_gain,
    weight_t,
    kvr,
    keys,
    values,
    wo,
    wq,
    subs=2,
    subs2=2,
    block=512,
):
    tokens, width = hidden.shape
    beams, cols = state.shape
    bf16, f32 = jnp.bfloat16, jnp.float32
    heads_here = width // DH
    split_at = (heads_here + 1) // 2
    wide_a, wide_b = split_at * DH, (heads_here - split_at) * DH
    rows = beams // n_tok
    state3 = state.reshape(n_head, beams // n_head, cols)
    pieces = (2, subs, tokens // 2 // subs, width)
    pieces2 = (2, subs2, tokens // subs2, 2 * DH)
    box = (n_tok, 2 * PAGE, DH)
    smem = pl.BlockSpec(memory_space=pltpu.SMEM)
    any_spec = pl.BlockSpec(memory_space=pl.ANY)
    vmem, dma = pltpu.VMEM, pltpu.SemaphoreType.DMA
    return pl.pallas_call(
        functools.partial(rest_kernel, n_tok, n_head, subs, subs2, block, split_at),
        out_shape=[
            jax.ShapeDtypeStruct(hidden.shape, bf16),
            jax.ShapeDtypeStruct(box, bf16),
            jax.ShapeDtypeStruct(state3.shape, bf16),
        ],
        in_specs=[smem] * 2 + [VMEM_SPEC] * 6 + [any_spec] * 6,
        out_specs=[VMEM_SPEC] * 3,
        scratch_shapes=[
            vmem((n_head, width, width), bf16),
            vmem((n_head, tokens, width), f32),
            vmem((n_head - 1, *pieces), bf16),
            vmem((n_head - 1, *pieces), bf16),
            vmem((n_head, tokens, 2 * DH), f32),
            vmem((n_head // 2, *pieces2), bf16),
            vmem((n_head // 2, *pieces2), bf16),
            vmem((n_head, 8, tokens), f32),
            vmem(kvr.shape, bf16),
            vmem((n_head, width, 2 * DH), bf16),
            vmem((2 * width, DH), f32),
            vmem(keys.shape, bf16),
            vmem(values.shape, bf16),
            vmem(wo.shape, bf16),
            vmem(wq.shape, bf16),
            vmem((1, keys.shape[0]), f32),
            vmem((heads_here, beams, 2 * DH), f32),
            vmem((heads_here, beams, DH), f32),
            vmem((tokens, DH), bf16),
            vmem((tokens, DH), bf16),
            vmem(box, bf16),
            vmem(box, bf16),
            vmem(box, bf16),
            vmem((beams, DH), f32),
            vmem((LAYERS, n_tok, rows, wide_a + DH), bf16),
            vmem((LAYERS, n_tok, rows, wide_b + DH), bf16),
            vmem((LAYERS, n_tok, rows, wide_a + DH), bf16),
            vmem((LAYERS, n_tok, rows, wide_b + DH), bf16),
            vmem((LAYERS, n_tok, rows, wide_a), bf16),
            vmem((LAYERS, n_tok, rows, wide_b), bf16),
            vmem((LAYERS, *state3.shape), bf16),
            vmem((LAYERS, *state3.shape), bf16),
            vmem((LAYERS, *state3.shape), bf16),
            vmem((n_tok, rows, width + DH), bf16),
            vmem((n_tok, rows, width + DH), bf16),
            vmem((n_tok, rows, wide_a), bf16),
            vmem((n_tok, rows, wide_b), bf16),
            dma((5,)),
            dma((n_head,)),
            dma((n_head - 1, 2, subs)),
            dma((n_head - 1, 2, subs)),
            dma((n_head // 2, 2, subs2)),
            dma((n_head // 2, 2, subs2)),
            dma((2,)),
            dma((2,)),
            dma((LAYERS + 1, 4, 2)),
            dma((LAYERS, 2, 2)),
        ],
        compiler_params=pltpu.CompilerParams(
            collective_id=2, has_side_effects=True, vmem_limit_bytes=56 << 20
        ),
        name="rest",
    )(
        page_home,
        cache_len,
        attended,
        hidden,
        gain[None, :],
        q,
        state3,
        beam_gain,
        weight_t,
        kvr,
        keys,
        values,
        wo,
        wq,
    )


def entry_kernel(
    n_tok,
    n_head,
    side,
    state_ref,
    gain_ref,
    wq_ref,
    query_ref,
    own_w,
    own_kv,
    kvw,
    cache,
    q_out_ref,
    att_ref,
    whole_w,
    kvr,
    keys_out,
    values_out,
    base_out,
    win,
    cache_v,
    keys,
    values,
    spread,
    q_send,
    q_recv,
    q_held,
    q_sems,
    w_sems,
    pair_sems,
    win_sems,
    kv_sems,
    kv_pair_sems,
    local_sems,
):
    me = lax.axis_index("tokens")
    me_h = lax.axis_index("heads")
    core = lax.rem(me, 2)
    y = lax.rem(me // 2, side)
    x = me // (2 * side)
    wide = n_tok // (2 * side)
    partner = me + 1 - 2 * core
    at = lambda i, j: (
        lax.rem(x + i + 2 * wide, wide) * side + lax.rem(y + j + 2 * side, side)
    ) * 2 + core
    cache_in = pltpu.make_async_copy(cache, cache_v, local_sems.at[3])
    cache_in.start()
    greet("tokens", n_tok, me)
    greet("heads", n_head, me_h)
    pl.semaphore_wait(pltpu.get_barrier_semaphore(), n_tok + n_head - 2)

    state = state_ref[...].astype(jnp.float32)
    squares = jnp.sum(state * state, axis=1, keepdims=True)
    scaled = (state * gain_ref[...].astype(jnp.float32)).astype(jnp.bfloat16)
    part = jnp.dot(scaled, wq_ref[...], preferred_element_type=jnp.float32)
    width = part.shape[1]
    rows = part.shape[0] // n_tok
    q_send[:, :, :width] = part.reshape(n_tok, rows, width).astype(jnp.bfloat16)
    q_send[:, :, width:] = (
        jnp.broadcast_to(squares, (part.shape[0], DH)).reshape(n_tok, rows, DH).astype(jnp.bfloat16)
    )
    scatter_start(q_send, q_recv, q_sems.at[0], "tokens", n_tok, me)
    q_recv[me] = q_send[me]

    def remote(src, dst, sems, target, axis="tokens"):
        return pltpu.make_async_remote_copy(
            src_ref=src,
            dst_ref=dst,
            send_sem=sems.at[0],
            recv_sem=sems.at[1],
            device_id={axis: target},
            device_id_type=MESH,
        )

    back = lambda b: lax.rem(me - b + n_tok, n_tok)
    ahead = lambda b: lax.rem(me + b, n_tok)
    win_two = remote(own_kv, win.at[2], win_sems.at[0], ahead(2))
    win_four = remote(own_kv, win.at[4], win_sems.at[1], ahead(4))
    win_two.start()
    win_four.start()

    depth = own_w.shape[0]
    piece = depth // 4
    block = lambda half, i, j: at(i, j) if half == 0 else at(j, i)

    def rows_of(half, part_at=None):
        if part_at is None:
            return pl.ds(half * 2 * piece, 2 * piece)
        return pl.ds((half * 2 + part_at) * piece, piece)

    slots = {}
    for half in (0, 1):
        for name in ("a+", "a-", "f+", "f-"):
            slots[half, name] = len(slots)
        for i in (0, -1, 1, 2):
            for name in ("a+", "a-", "f+", "f-"):
                slots[half, i, name] = len(slots)

    def first(half, name):
        way = 1 if name[1] == "+" else -1
        target = block(half, way, 0)
        if name[0] == "a":
            where = rows_of(half)
            return remote(
                own_w.at[where], whole_w.at[me, where], w_sems.at[slots[half, name]], target
            )
        ref = whole_w.at[block(half, -way, 0), rows_of(half, 0 if way == 1 else 1)]
        return remote(ref, ref, w_sems.at[slots[half, name]], target)

    def first_in(half, name):
        way = 1 if name[1] == "+" else -1
        if name[0] == "a":
            ref = whole_w.at[block(half, -way, 0), rows_of(half)]
        else:
            ref = whole_w.at[block(half, -2 * way, 0), rows_of(half, 0 if way == 1 else 1)]
        return remote(ref, ref, w_sems.at[slots[half, name]], block(half, way, 0))

    def second(half, i, name):
        way = 1 if name[1] == "+" else -1
        target = block(half, 0, way)
        if name[0] == "a":
            where = rows_of(half)
            dst = whole_w.at[block(half, i, 0), where]
            src = own_w.at[where] if i == 0 else dst
        else:
            src = dst = whole_w.at[block(half, i, -way), rows_of(half, 0 if way == 1 else 1)]
        return remote(src, dst, w_sems.at[slots[half, i, name]], target)

    def second_in(half, i, name):
        way = 1 if name[1] == "+" else -1
        if name[0] == "a":
            ref = whole_w.at[block(half, i, -way), rows_of(half)]
        else:
            ref = whole_w.at[block(half, i, -2 * way), rows_of(half, 0 if way == 1 else 1)]
        return remote(ref, ref, w_sems.at[slots[half, i, name]], block(half, 0, way))

    def share(half, i, j):
        where = rows_of(half)
        dst = whole_w.at[block(half, i, j), where]
        src = own_w.at[where] if (i, j) == (0, 0) else dst
        remote(src, dst, pair_sems, partner).start()

    halves = (0, 1)
    for half in halves:
        for name in ("a+", "a-"):
            first(half, name).start()
    for half in halves:
        for name in ("a+", "a-"):
            second(half, 0, name).start()
    for half in halves:
        share(half, 0, 0)

    kv_rows = kvw.shape[1] // 2
    kv_half = pl.ds(pl.multiple_of(core * kv_rows, kv_rows), kv_rows)

    def kv_out(k):
        target = lax.rem(me_h + k, n_head)
        return remote(
            kvw.at[target, kv_half], kvr.at[me_h, kv_half], kv_sems.at[k - 1], target, "heads"
        )

    def kv_in(k):
        ref = kvr.at[lax.rem(me_h - k + n_head, n_head), kv_half]
        return remote(ref, ref, kv_sems.at[k - 1], lax.rem(me_h + k, n_head), "heads")

    order = sorted(range(1, n_head), key=lambda k: min(k, n_head - k))
    for k in order:
        kv_out(k).start()

    own_copies = [
        pltpu.make_async_copy(own_w, whole_w.at[me], local_sems.at[0]),
        pltpu.make_async_copy(own_kv, win.at[0], local_sems.at[1]),
        pltpu.make_async_copy(kvw.at[me_h], kvr.at[me_h], local_sems.at[2]),
    ]
    for copy in own_copies:
        copy.start()

    finish(q_recv, q_sems.at[0], "tokens", n_tok, me)
    total = jnp.sum(q_recv[...].astype(jnp.float32), axis=0)
    factor = lax.rsqrt(total[:, width : width + 1] / D + EPSILON)
    q_held[me] = (total[:, :width] * factor).astype(jnp.bfloat16)
    gather_start(q_held, q_sems.at[1], "tokens", n_tok, me)

    own_copies[1].wait()
    cache_in.wait()
    base_copy = pltpu.make_async_copy(cache_v, base_out, local_sems.at[4])
    base_copy.start()
    parts = cache_v.shape[0] // spread.shape[0]

    def split(k):
        size = spread.shape[0]
        spread[...] = cache_v[k * size : (k + 1) * size, :].astype(jnp.float32)
        at = slice(k * size // 2, (k + 1) * size // 2)
        keys[at, :] = spread[pl.ds(0, size // 2, stride=2), :].astype(jnp.bfloat16)
        values[at, :] = spread[pl.ds(1, size // 2, stride=2), :].astype(jnp.bfloat16)

    def attend_window(g):
        cols = slice(g * DH, (g + 1) * DH)
        q = query_ref[:, cols]
        count = q.shape[0]
        acc = jnp.zeros((count, 2 * DH), jnp.float32)
        top = jnp.full((count, 1), -1e30, jnp.float32)
        row = lax.broadcasted_iota(jnp.int32, (count, count), 0)
        col = lax.broadcasted_iota(jnp.int32, (count, count), 1)
        ones = jnp.ones((count, DH), jnp.bfloat16)
        reach = win.shape[0]
        for b in range(reach):
            s = lax.dot_general(
                q, win[b, 0], (((1,), (1,)), ((), ())), preferred_element_type=jnp.float32
            )
            if b == 0:
                s = jnp.where(col <= row, s, -1e30)
            else:
                s = s + jnp.where(me >= b, jnp.float32(0.0), jnp.float32(-1e30))
            if b == reach - 1:
                s = jnp.where(col > row, s, -1e30)
            here = jnp.maximum(top, jnp.max(s, axis=1, keepdims=True))
            p = jnp.exp2((s - here) * SCALE2).astype(jnp.bfloat16)
            shrink = jnp.exp2((top - here) * SCALE2)
            both = jnp.concatenate([win[b, 1], ones], axis=1)
            acc = acc * shrink + jnp.dot(p, both, preferred_element_type=jnp.float32)
            top = here
        att_ref[:, cols] = (acc[:, :DH] / acc[:, DH:]).astype(jnp.bfloat16)

    early = [functools.partial(split, k) for k in range(parts)]
    late = [functools.partial(attend_window, g) for g in range(query_ref.shape[1] // DH)]

    def fill(work, amount=1):
        for _ in range(amount):
            if work:
                work.pop(0)()

    win_in = lambda b, k: remote(win.at[b], win.at[b], win_sems.at[k], partner)

    def relay(src, dst, k):
        return remote(win.at[src], win.at[dst], win_sems.at[k], partner)

    for name in ("a+", "a-"):
        way = 1 if name[1] == "+" else -1
        for half in halves:
            first_in(half, name).wait_recv()
            first(half, "f" + name[1]).start()
            for other in ("a+", "a-"):
                second(half, -way, other).start()
            share(half, -way, 0)
        fill(early)
    win_in(2, 0).wait_recv()
    relay(2 * core, 1, 2).start()
    for name in ("a+", "a-"):
        way = 1 if name[1] == "+" else -1
        for half in halves:
            second_in(half, 0, name).wait_recv()
            second(half, 0, "f" + name[1]).start()
            share(half, 0, -way)
        fill(early)
    for half in halves:
        first_in(half, "f+").wait_recv()
        first_in(half, "f-").wait_recv()
        for other in ("a+", "a-"):
            second(half, 2, other).start()
        share(half, 2, 0)
    win_in(4, 1).wait_recv()
    relay(2 + 2 * core, 3, 3).start()
    for i in (-1, 1):
        for name in ("a+", "a-"):
            way = 1 if name[1] == "+" else -1
            for half in halves:
                second_in(half, i, name).wait_recv()
                second(half, i, "f" + name[1]).start()
                share(half, i, -way)
            fill(early)
    fill(early, parts)
    keys_copy = pltpu.make_async_copy(keys, keys_out, local_sems.at[5])
    values_copy = pltpu.make_async_copy(values, values_out, local_sems.at[6])
    keys_copy.start()
    values_copy.start()
    win_in(1, 2).wait_recv()
    win_in(3, 3).wait_recv()
    finish(q_held, q_sems.at[1], "tokens", n_tok, me)
    q_out_ref[...] = q_held[...].astype(jnp.float32).reshape(-1, width).astype(jnp.bfloat16)

    def kv_share(k):
        ref = kvr.at[lax.rem(me_h - k + n_head, n_head), kv_half]
        return remote(ref, ref, kv_pair_sems.at[k - 1], partner)

    def kv_share_in(k):
        other = pl.ds(pl.multiple_of((1 - core) * kv_rows, kv_rows), kv_rows)
        ref = kvr.at[lax.rem(me_h - k + n_head, n_head), other]
        return remote(ref, ref, kv_pair_sems.at[k - 1], partner)

    for k in order[: n_head // 2]:
        kv_in(k).wait_recv()
        kv_share(k).start()
    fill(late)
    for half in halves:
        second_in(half, 0, "f+").wait_recv()
        second_in(half, 0, "f-").wait_recv()
        share(half, 0, 2)
    for name in ("a+", "a-"):
        way = 1 if name[1] == "+" else -1
        for half in halves:
            second_in(half, 2, name).wait_recv()
            second(half, 2, "f" + name[1]).start()
            share(half, 2, -way)
        fill(late)
    for i in (-1, 1, 2):
        for half in halves:
            second_in(half, i, "f+").wait_recv()
            second_in(half, i, "f-").wait_recv()
            share(half, i, 2)
        if i != 2:
            fill(late)
    fill(late, len(late))
    for k in order[n_head // 2 :]:
        kv_in(k).wait_recv()
        kv_share(k).start()

    relay(2 * core, 1, 2).wait_send()
    relay(2 + 2 * core, 3, 3).wait_send()
    win_two.wait_send()
    win_four.wait_send()
    for half in halves:
        for name in ("a+", "a-", "f+", "f-"):
            first(half, name).wait_send()
            for i in (0, -1, 1, 2):
                second(half, i, name).wait_send()
    for k in order:
        kv_out(k).wait_send()
        kv_share(k).wait_send()
        kv_share_in(k).wait_recv()
    half_of_all = whole_w.at[pl.ds(0, n_tok // 2)]
    remote(half_of_all, half_of_all, pair_sems, partner).wait()
    own_copies[0].wait()
    own_copies[2].wait()
    base_copy.wait()
    keys_copy.wait()
    values_copy.wait()


def entry(n_tok, n_head, state, gain, wq, queries, own_w, own_kv, kvw, cache, side=4):
    bf16 = jnp.bfloat16
    half_cache = (cache.shape[0] // 2, DH)
    beams = state.shape[0]
    width = wq.shape[1]
    rows = beams // n_tok
    any_spec = pl.BlockSpec(memory_space=pl.ANY)
    reach = WINDOW // own_kv.shape[1] + 1
    return pl.pallas_call(
        functools.partial(entry_kernel, n_tok, n_head, side),
        out_shape=[
            jax.ShapeDtypeStruct((beams, width), bf16),
            jax.ShapeDtypeStruct(queries.shape, bf16),
            jax.ShapeDtypeStruct((n_tok, *own_w.shape), bf16),
            jax.ShapeDtypeStruct(kvw.shape, bf16),
            jax.ShapeDtypeStruct(half_cache, bf16),
            jax.ShapeDtypeStruct(half_cache, bf16),
            jax.ShapeDtypeStruct(cache.shape, bf16),
        ],
        in_specs=[VMEM_SPEC] * 4 + [any_spec] * 4,
        out_specs=[VMEM_SPEC] * 2 + [any_spec] * 5,
        scratch_shapes=[
            pltpu.VMEM((reach, *own_kv.shape), bf16),
            pltpu.VMEM(cache.shape, bf16),
            pltpu.VMEM(half_cache, bf16),
            pltpu.VMEM(half_cache, bf16),
            pltpu.VMEM((cache.shape[0] // 8, DH), jnp.float32),
            pltpu.VMEM((n_tok, rows, width + DH), bf16),
            pltpu.VMEM((n_tok, rows, width + DH), bf16),
            pltpu.VMEM((n_tok, rows, width), bf16),
            pltpu.SemaphoreType.DMA((2, 2)),
            pltpu.SemaphoreType.DMA((40, 2)),
            pltpu.SemaphoreType.DMA((2,)),
            pltpu.SemaphoreType.DMA((4, 2)),
            pltpu.SemaphoreType.DMA((n_head - 1, 2)),
            pltpu.SemaphoreType.DMA((n_head - 1, 2)),
            pltpu.SemaphoreType.DMA((7,)),
        ],
        compiler_params=pltpu.CompilerParams(
            collective_id=1, has_side_effects=True, vmem_limit_bytes=24 << 20
        ),
        name="entry",
    )(state, gain, wq, queries, own_w, own_kv, kvw, cache)


def place_kernel(n_tok, own_pages, home_ref, base_ref, inbox_ref, out_ref, sem):
    me = lax.axis_index("tokens")
    rows = inbox_ref.shape[1]
    pages_here = out_ref.shape[0] // rows

    def each(act):
        def one(slot, carry):
            page = page_slot(home_ref, me, own_pages, pages_here, n_tok, slot)

            @pl.when(page >= 0)
            def _():
                at = pl.ds(pl.multiple_of(page * rows, rows), rows)
                act(pltpu.make_async_copy(inbox_ref.at[slot], out_ref.at[at], sem))

            return carry

        lax.fori_loop(0, n_tok, one, 0)

    each(lambda copy: copy.start())
    each(lambda copy: copy.wait())


def place_pages(n_tok, own_pages, page_home, base, inbox):
    return pl.pallas_call(
        functools.partial(place_kernel, n_tok, own_pages),
        out_shape=jax.ShapeDtypeStruct(base.shape, base.dtype),
        in_specs=[
            pl.BlockSpec(memory_space=pltpu.SMEM),
            pl.BlockSpec(memory_space=pl.ANY),
            VMEM_SPEC,
        ],
        out_specs=pl.BlockSpec(memory_space=pl.ANY),
        scratch_shapes=[pltpu.SemaphoreType.DMA],
        input_output_aliases={1: 0},
        name="place_pages",
    )(page_home, base, inbox)


def shards(
    hidden_in,
    queries,
    keyvals,
    out_weight,
    kv_gain,
    kv_weight,
    cache,
    page_home,
    cache_len,
    beam_state,
    parents,
    beam_gain,
    query_weight,
    beam_out_weight,
):
    n_tok = lax.axis_size("tokens")
    n_head = lax.axis_size("heads")
    state = jnp.take(beam_state, parents, axis=0)
    q, attended, weight_t, kvr, keys, values, base = entry(
        n_tok,
        n_head,
        state,
        beam_gain[0:1],
        query_weight[0],
        queries,
        out_weight.T,
        jnp.swapaxes(keyvals, 0, 1),
        kv_weight.reshape(n_head, -1, DH),
        cache.reshape(-1, DH),
    )
    stretch_hidden, inbox, beams_out = rest(
        n_tok,
        n_head,
        page_home,
        cache_len,
        attended,
        hidden_in,
        kv_gain,
        q,
        state,
        beam_gain[1:2],
        weight_t.reshape(-1, weight_t.shape[2]),
        kvr,
        keys,
        values,
        jnp.swapaxes(beam_out_weight, 1, 2),
        query_weight[1],
    )
    new_cache = place_pages(n_tok, hidden_in.shape[0] // PAGE, page_home, base, inbox)
    return (stretch_hidden, new_cache.reshape(cache.shape), beams_out.reshape(state.shape))


def solution(mesh):
    tokens = "tokens"
    placed = (
        P(tokens, "heads"),
        P(tokens, "heads"),
        P(tokens, None, "heads"),
        P("heads", tokens),
        P("heads"),
        P(None, None, "heads"),
        P(tokens, None, "heads"),
        P(),
        P(),
        P(None, tokens),
        P(),
        P(None, tokens),
        P(None, tokens, "heads"),
        P(None, "heads", tokens),
    )
    return jax.shard_map(
        shards,
        mesh=mesh,
        in_specs=placed,
        out_specs=(P(tokens, "heads"), P(tokens, None, "heads"), P(None, tokens)),
        check_vma=False,
    )
```

time: 262 us -> 209 us (0.80)
  local copies, waits for them, and re-layouts: 49.4 us -> 24.9 us
  Pallas kernels: 203 us -> 180 us
  between operations: 4.32 us -> 1.53 us
    pallas_call x8 -> x2, Pallas kernels: 156 us -> 133 us  [the longest x1 130 us: rest(): pl.pallas_call(functools.partial(rest_kernel, n_tok, n_head, subs, subs2,...]
    unnamed x91 -> x31, local copies, waits for them, and re-layouts: 33.8 us -> 19.3 us
    reshape x2 -> x0, local copies, waits for them, and re-layouts: 5.87 us -> none  [the longest x1 4.16 us: shards(): kv_weight.reshape(n_head, -1, 2 * DH)]
    slice x4 -> x0, local copies, waits for them, and re-layouts: 4.47 us -> none  [the longest x1 2.98 us: shards(): old_values = jnp.concatenate([cache[:, 1], jnp.ones_like(old_keys)], axis=1)]
where the time goes in v3:
time: 209 us
  Pallas kernels  180 us (86%)
  local copies, waits for them, and re-layouts  24.9 us (12%)
  other arithmetic  2.31 us (1%)
    pallas_call x1, Pallas kernels, rest(): pl.pallas_call(functools.partial(rest_kernel, n_tok, n_head, subs, subs2,...  130 us
    pallas_call x1, Pallas kernels, entry(): pl.pallas_call(functools.partial(entry_kernel, n_tok, n_head, side), out_...  47.3 us
    unnamed x31, local copies, waits for them, and re-layouts  19.3 us

profile of v3, /device:TPU:1, one launch (start us, length us, event | category | flops | bytes accessed | tf_op | source)
XLA Modules:
  0.0 208.7 jit_solution(3566292171058649239)
XLA Ops:
  0.6 0.0 copy-start.2
  0.6 0.0 copy-start.7
  1.4 0.8 compare_and_fusion
  2.2 0.1 broadcast_in_dim.25
  2.3 0.7 compare_select_fusion
  3.0 1.3 fusion
  4.3 1.3 broadcast_in_dim.24.gain_ref
  5.6 0.9 copy.22
  6.5 1.0 copy.18
  7.5 1.2 gather_fusion
  8.7 0.7 broadcast_select_fusion.1.state_ref
  9.4 0.1 broadcast_select_fusion.state_ref
  9.5 1.8 slice_bitcast_fusion
  11.3 0.0 copy-done.2
  11.3 0.0 copy-done.7
  11.3 0.0 copy-start.4
  11.3 1.6 copy-done.4
  12.9 0.0 copy-start.10
  12.9 0.9 copy-done.10
  13.8 47.3 %entry.1 = (bf16[256,640]{1,0:T(8,128)(2,1)S(1)}, bf16[256,640]{1,0:T(8,128)(2,1)S(1)}, bf16[32,160,640]{2,1,0:T(8,128)(2,1)S(1)}, bf16[8,1280,128]{2,1,0:T(8,12...) custom-call(bf16[256,160]{1,0:T(8,128)(2,1)S(1)} %broadcast_select_fusion.s, ...), custom_call_target="tpu_custom_call" | custom-call | tf_op jit(solution)/shard_map/entry/pallas_call | solution.py:963
  61.1 0.0 copy-start
  61.1 1.3 copy-done
  62.4 0.0 copy-start.1
  62.4 2.7 %copy-done.1 = bf16[32,160,640]{2,1,0:T(8,128)(2,1)} copy-done((bf16[32,160,640]{2,1,0:T(8,128)(2,1)}, bf16[32,160,640]{2,1,0:T(8,128)(2,1)S(1)}, u32[]{:S(2)}) %copy-start.1) | copy-done | bytes 6553624
  65.1 0.0 copy-start.3
  65.1 1.5 copy-done.3
  66.7 0.0 copy-start.5
  66.7 1.0 copy-done.5
  67.6 0.0 copy-start.6
  67.6 1.0 copy-done.6
  68.6 0.0 copy-start.8
  68.6 0.8 copy-done.8
  69.4 0.0 copy-start.9
  69.4 0.7 copy-done.9
  70.1 130.2 %rest.1 = (bf16[256,640]{1,0:T(8,128)(2,1)}, bf16[32,32,128]{2,1,0:T(8,128)(2,1)}, bf16[8,32,160]{2,1,0:T(8,128)(2,1)}) custom-call(s32[512]{0:T(512)} %home_ref.3, s32[1]{0:T(128)S(6)} %copy.26.len_ref, bf16[256,640]{1,0:T(8,128)(2,1)} %copy-done.9, bf16[256,640]{1,0:T(8,128)(2,1)} %hid_ref.1, bf16[1,640]{1,0:T(2,128)(2,1)} %broadcast_in_dim.24.gain_ref, ...), custom_call_target="tpu_custom_call" | custom-call | tf_op jit(solution)/shard_map/rest/pallas_call | solution.py:536
  200.3 0.0 copy-start.12
  200.3 0.0 copy-start.11
  200.3 2.5 %place_pages.1 = bf16[8192,128]{1,0:T(8,128)(2,1)} custom-call(s32[512]{0:T(512)} %home_ref.3, bf16[8192,128]{1,0:T(8,128)(2,1)} %copy-done, bf16[32,32,128]{2,1,0:T(8,128)(2,1)} %get-tuple-element.21.inbox_ref), custom_call_target="tpu_custom_call", output_to_operand_aliasing={{}: (1, {})} | custom-call | tf_op jit(solution)/shard_map/place_pages/pallas_call | solution.py:1023
  202.8 0.0 copy-done.12
  202.8 0.7 copy.20
  203.6 0.0 copy-done.11
  203.6 0.7 copy.27
  204.3 4.4 %copy.28 = bf16[4096,2,128]{2,1,0:T(2,128)(2,1)} copy(bf16[4096,2,128]{2,1,0:T(2,128)(2,1)} %bitcast.15) | data formatting | bytes 4194304
  (1 shorter events, 0.0 us)
Async XLA Ops:
  0.6 10.7 %copy-start.2 = (bf16[5120,2,128]{2,1,0:T(2,128)(2,1)S(1)}, bf16[5120,2,128]{2,1,0:T(2,128)(2,1)}, u32[]{:S(2)}) copy-start(bf16[5120,2,128]{2,1,0:T(2,128)(2,1)} %param.19) | copy-start | bytes 7864324
  0.6 10.6 %copy-start.7 = (bf16[256,640]{1,0:T(8,128)(2,1)S(1)}, bf16[256,640]{1,0:T(8,128)(2,1)}, u32[]{:S(2)}) copy-start(bf16[256,640]{1,0:T(8,128)(2,1)} %query_ref.1) | copy-start | bytes 983044
  11.3 1.6 copy-start.4
  12.9 0.9 copy-start.10
  61.1 1.3 copy-start
  62.4 2.7 %copy-start.1 = (bf16[32,160,640]{2,1,0:T(8,128)(2,1)}, bf16[32,160,640]{2,1,0:T(8,128)(2,1)S(1)}, u32[]{:S(2)}) copy-start(bf16[32,160,640]{2,1,0:T(8,128)(2,1)S(1)} %get-tuple-element.15) | copy-start | bytes 19660804
  65.1 1.5 copy-start.3
  66.7 1.0 copy-start.5
  67.6 1.0 copy-start.6
  68.6 0.8 copy-start.8
  69.4 0.7 copy-start.9
  200.3 2.5 %copy-start.12 = (bf16[8,32,160]{2,1,0:T(8,128)(2,1)S(1)}, bf16[8,32,160]{2,1,0:T(8,128)(2,1)}, u32[]{:S(2)}) copy-start(bf16[8,32,160]{2,1,0:T(8,128)(2,1)} %get-tuple-element.22) | copy-start | bytes 245764
  200.3 3.3 %copy-start.11 = (bf16[256,640]{1,0:T(8,128)(2,1)S(1)}, bf16[256,640]{1,0:T(8,128)(2,1)}, u32[]{:S(2)}) copy-start(bf16[256,640]{1,0:T(8,128)(2,1)} %get-tuple-element.33) | copy-start | bytes 983044
